TPU v7x, 128 devices: a whole 4x4x4 slice. The times are simulated.
128 devices in a mesh: dp: 4 (over x), tm: 32 (over z, y, core).
Axes of the slice: x: 4, y: 4, z: 4, core: 2. Of those that a mesh axis runs over, the one named last changes fastest.
Arguments:
- clips: bfloat16 [4, 512, 512, 512], P('dp', 'tm'), may hold values from -6 to 6
- w_time: bfloat16 [3, 512, 512], P(None, 'dp'), may hold values from -0.15625 to 0.15625
- gain: float32 [512], replicated, may hold values from 0.1 to 1.9
- rate: float32 [512], replicated, may hold values from 9.765625e-05 to 0.0333333333
- keep: float32 [512], P('tm'), may hold values from 0.5 to 1
- latent_ids: int32 [512], P('tm'), may hold values from 0 to 63, as said below
- w_lat: bfloat16 [512, 16], replicated, may hold values from -0.25 to 0.25
Outputs:
- features: bfloat16 [4, 512, 512, 512], P('dp', 'tm')
- latents: float32 [4, 64, 16, 512], P('dp', 'tm')
Inputs may be any that keep to these rules, and one draw needn't show every extreme that they name: latent_ids never falls as the frame grows; latent frame j begins at a frame from j * 8 - 7 to j * 8 (latent 0 at frame 0) and ends where the next begins; every latent frame gets 1 to 15 frames and the last exactly 15.
All inputs are finite; a program needn't handle non-finite values.
Results may differ from a plain program's by a relative error of at most 0.0025.
Values may be sent and summed in bfloat16 or wider, within the bound.
No kernel may reach another device: no remote copies, remote signals or barrier semaphores. Data moves between devices by JAX's collectives and lax.ppermute only.
A program may use at most 192 MiB of HBM per device.

v0:
```python
import functools

import jax
import jax.numpy as jnp
from jax import lax
from jax.experimental import pallas as pl
from jax.experimental.pallas import tpu as pltpu
from jax.sharding import PartitionSpec as P


KT = 3
STRIDE = 8
F32 = jnp.float32
BF16 = jnp.bfloat16
CHUNKS = (256, 256)
SUB = 16


def rotated(value, axis, steps):
    count = lax.axis_size(axis)
    return lax.ppermute(value, axis, [(s, (s + steps) % count) for s in range(count)])


def shifted(value, axis, steps):
    count = lax.axis_size(axis)
    return lax.ppermute(value, axis, [(s, s + steps) for s in range(count - steps)])


def swapped(value, axis):
    return lax.ppermute(value, axis, [(s, s ^ 1) for s in range(lax.axis_size(axis))])


def conv_kernel(window, keep, x_hbm, halo_hbm, own, da, db, dc, sa, sb, sc, decay, *rest, start, width, shards):
    feat_hbm, last, pooled, w, X, H, F, wsem, insem, outsem = rest[-10:]
    nframe = x_hbm.shape[0]
    half = da.shape[1]
    depth = own.shape[1]
    me = lax.axis_index("dp")
    side = lax.rem(lax.axis_index("tm"), 2)

    def weights():
        copies = [pltpu.make_async_copy(own, w.at[:, pl.ds(pl.multiple_of(me * depth, depth), depth)], wsem.at[0])]
        slot = 1
        for step, mine, other in ((shards - 1, da, sa), (1, db, sb), (2, dc, sc)):
            base = lax.rem(me + step, shards) * depth
            for piece, lane in ((mine, side), (other, 1 - side)):
                row = pl.multiple_of(base + lane * half, half)
                copies.append(pltpu.make_async_copy(piece, w.at[:, pl.ds(row, half)], wsem.at[slot]))
                slot += 1
        return copies

    def prior(f):
        return pltpu.make_async_copy(halo_hbm.at[f, pl.ds(start, width)], X.at[f], insem.at[f])

    def entering(f):
        return pltpu.make_async_copy(x_hbm.at[f, pl.ds(start, width)], X.at[f + KT - 1], insem.at[f + KT - 1])

    def leaving(f, slot):
        return pltpu.make_async_copy(F.at[slot], feat_hbm.at[f, pl.ds(start, width)], outsem.at[slot])

    def product(f, slot):
        nchan = w.shape[2]
        for n in range(0, nchan, 256):
            total = None
            for k in range(KT):
                part = jnp.dot(X[f + KT - 1 - k], w[k, :, n : n + 256], preferred_element_type=F32)
                total = part if total is None else total + part
            H[slot, :, n : n + 256] = total

    def finish(f, slot):
        j = window[f]
        kept = decay[...] * keep[f]
        nchan = w.shape[2]
        for r in range(0, width, SUB):
            h = H[slot, r : r + SUB, :]
            c = X[f + KT - 1, r : r + SUB, :].astype(F32)
            rounded = (c + (h + h * jnp.tanh(h))).astype(BF16)
            F[slot, r : r + SUB, :] = rounded
            v = rounded.astype(F32)
            scale = lax.rsqrt(jnp.sum(v * v, -1, keepdims=True) * (1.0 / nchan) + 1e-06)
            state = last[r : r + SUB, :] * kept + v * scale
            last[r : r + SUB, :] = state
            pooled[j, r : r + SUB, :] += state

    pieces = weights()
    for copy in pieces:
        copy.start()
    for f in range(KT - 1):
        prior(f).start()
    for f in range(nframe):
        entering(f).start()
    last[...] = jnp.zeros_like(last)
    pooled[...] = jnp.zeros_like(pooled)
    for copy in pieces:
        copy.wait()
    for f in range(KT - 1):
        prior(f).wait()
    entering(0).wait()
    product(0, 0)

    def body(f, _):
        slot = lax.rem(f, 2)

        @pl.when(f >= 2)
        def _():
            leaving(f - 2, slot).wait()

        entering(f + 1).wait()
        product(f + 1, 1 - slot)
        finish(f, slot)
        leaving(f, slot).start()
        return 0

    lax.fori_loop(0, nframe - 1, body, 0)
    final = (nframe - 1) % 2
    leaving(nframe - 3, final).wait()
    finish(nframe - 1, final)
    leaving(nframe - 1, final).start()
    leaving(nframe - 2, 1 - final).wait()
    leaving(nframe - 1, final).wait()


def table_kernel(packed, rate, scaled, high, low, counts, E):
    nall, lanes = packed.shape
    nchan = rate.shape[1]
    nlat = high.shape[0]
    me = lax.axis_index("tm")
    end = (me + 1) * (nall // lax.axis_size("tm")) - 1
    frame = lax.broadcasted_iota(jnp.int32, (nall, lanes), 0)
    logs = jnp.where(frame > end, jnp.log(jnp.maximum(packed[...], 0.5)), 0.0)
    rows = lax.broadcasted_iota(jnp.int32, (nall, nall), 0)
    cols = lax.broadcasted_iota(jnp.int32, (nall, nall), 1)
    run = jnp.dot(
        (cols <= rows).astype(F32), logs, precision=lax.Precision.HIGHEST, preferred_element_type=F32
    )
    block = 128
    for r in range(0, nall, block):
        at = lax.broadcasted_iota(jnp.int32, (block, nchan), 0) + r
        gap = (at - end).astype(F32)
        E[r : r + block, :] = jnp.where(at > end, jnp.exp(run[r : r + block, 0:1] - rate[...] * gap), 0.0)
    ids = packed[:, lanes // 2 : lanes // 2 + 1].astype(jnp.int32)
    member = (lax.broadcasted_iota(jnp.int32, (nall, lanes), 1) == ids).astype(F32)
    table = lax.dot_general(
        member, E[...], (((0,), (0,)), ((), ())), precision=lax.Precision.HIGHEST, preferred_element_type=F32
    )
    per = counts.shape[0]
    for i in range(per):
        hit = (jnp.broadcast_to(ids, (nall, lanes)) == me * per + i).astype(F32)
        counts[i : i + 1, :] = jnp.sum(hit, 0, keepdims=True)
    E[0:lanes, :] = table
    for j in range(nlat):
        value = scaled[...] * E[j : j + 1, :]
        upper = value.astype(BF16)
        high[j] = upper
        low[j] = (value - upper.astype(F32)).astype(BF16)


def times(a, b):
    return lax.dot_general(a, b, (((1,), (1,)), ((), ())), preferred_element_type=F32)


def split(value):
    upper = value.astype(BF16)
    return upper, (value - upper.astype(F32)).astype(BF16)


def spread_kernel(high, low, scaled, last, pooled, sends, own):
    nlat, nproj, nchan = high.shape
    ndev = sends.shape[0]
    width = last.shape[0]
    top, rest = split(last[...])
    rows = 256
    per = sends.shape[1]
    for r in range(0, nlat * nproj, rows):
        upper = high[r // nproj : (r + rows) // nproj].reshape(rows, nchan)
        lower = low[r // nproj : (r + rows) // nproj].reshape(rows, nchan)
        z = times(upper, top) + times(upper, rest) + times(lower, top)
        sends[r // per : (r + rows) // per] = z.reshape(rows // per, per, width).astype(BF16)
    upper, lower = split(scaled[...])
    parts = []
    for j in range(3):
        top, rest = split(pooled[j])
        parts.append(times(upper, top) + times(upper, rest) + times(lower, top))
    own[0:nproj, :] = parts[0]
    own[nproj : 2 * nproj, :] = parts[1]
    me = lax.axis_index("tm")

    @pl.when(me < ndev - 1)
    def _():
        block = sends[me + 1]
        sends[me + 1, 0:nproj] = (block[0:nproj].astype(F32) + parts[2]).astype(BF16)


def final_kernel(counts, *refs):
    per = counts.shape[0]
    latents = refs[-1]
    start = 0
    for index in range(len(refs) // 2):
        got, own = refs[2 * index], refs[2 * index + 1]
        ndev, rows, width = got.shape
        nproj = rows // per
        for i in range(per):
            part = slice(i * nproj, (i + 1) * nproj)
            total = own[part, :]
            for d in range(ndev):
                total = total + got[d, part, :].astype(F32)
            for n in range(0, width, 128):
                latents[i, :, start + n : start + n + 128] = total[:, n : n + 128] / counts[i : i + 1, :]
        start += width


def per_device(clips, w_time, gain, rate, keep, latent_ids, w_lat):
    _, nframe, npos, nchan = clips.shape
    nproj = w_lat.shape[1]
    ndev = lax.axis_size("tm")
    shards = lax.axis_size("dp")
    nall = nframe * ndev
    per = nframe // STRIDE
    nlat = per * ndev
    me = lax.axis_index("tm")
    side = me % 2
    x = clips[0]

    own_w = w_time * jnp.asarray(0.5, BF16)
    half = own_w.shape[1] // 2
    mine = lax.dynamic_slice_in_dim(own_w, side * half, half, 1)
    halo = shifted(x[nframe - (KT - 1) :], "tm", 1)
    da, db, dc = rotated(mine, "dp", 1), rotated(mine, "dp", -1), rotated(mine, "dp", 2)
    sa, sb, sc = swapped(da, "tm"), swapped(db, "tm"), swapped(dc, "tm")

    lane = jnp.arange(128, dtype=jnp.int32)[None]
    local = jnp.where(lane < 64, keep[:, None], latent_ids.astype(F32)[:, None])
    local = jnp.broadcast_to(local[None], (ndev, nframe, 128))
    packed = lax.all_to_all(local, "tm", 0, 0).reshape(nall, 128)

    decay = jnp.exp(-rate)[None]
    inject = jnp.sqrt(-jnp.expm1(-2.0 * rate))
    scaled = w_lat.T.astype(F32) * (inject * gain)[None]

    vmem = pl.BlockSpec(memory_space=pltpu.VMEM)
    smem = pl.BlockSpec(memory_space=pltpu.SMEM)
    hbm = pl.BlockSpec(memory_space=pltpu.HBM)
    table_shape = jax.ShapeDtypeStruct((nlat, nproj, nchan), BF16)

    window = latent_ids - me.astype(jnp.int32) * per
    features = None
    start = 0
    outs = []
    for index, width in enumerate(CHUNKS):
        before = () if features is None else (features,)
        conv = pl.pallas_call(
            functools.partial(conv_kernel, start=start, width=width, shards=shards),
            out_shape=(
                jax.ShapeDtypeStruct((nframe, npos, nchan), BF16),
                jax.ShapeDtypeStruct((width, nchan), F32),
                jax.ShapeDtypeStruct((3, width, nchan), F32),
            ),
            in_specs=[smem, smem] + [hbm] * 9 + [vmem] + [hbm] * len(before),
            out_specs=(hbm, vmem, vmem),
            input_output_aliases={12: 0} if before else {},
            scratch_shapes=[
                pltpu.VMEM((KT, nchan, nchan), BF16),
                pltpu.VMEM((nframe + KT - 1, width, nchan), BF16),
                pltpu.VMEM((2, width, nchan), F32),
                pltpu.VMEM((2, width, nchan), BF16),
                pltpu.SemaphoreType.DMA((7,)),
                pltpu.SemaphoreType.DMA((nframe + KT - 1,)),
                pltpu.SemaphoreType.DMA((2,)),
            ],
            cost_estimate=pl.CostEstimate(
                flops=2 * KT * nframe * width * nchan * nchan,
                bytes_accessed=4 * nframe * width * nchan,
                transcendentals=nframe * width * nchan,
            ),
        )
        features, last, pooled = conv(window, keep, x, halo, own_w, da, db, dc, sa, sb, sc, decay, *before)
        if index == 0:
            packed, last = lax.optimization_barrier((packed, last))
            high, low, counts = pl.pallas_call(
                table_kernel,
                out_shape=(table_shape, table_shape, jax.ShapeDtypeStruct((per, 128), F32)),
                in_specs=[vmem] * 3,
                out_specs=(vmem,) * 3,
                scratch_shapes=[pltpu.VMEM((nall, nchan), F32)],
                compiler_params=pltpu.CompilerParams(vmem_limit_bytes=24 << 20),
                cost_estimate=pl.CostEstimate(
                    flops=12 * nlat * nall * nchan, bytes_accessed=4 << 20, transcendentals=nall * nchan
                ),
                name="tables",
            )(packed, rate[None], scaled)
        sends, own = pl.pallas_call(
            spread_kernel,
            out_shape=(
                jax.ShapeDtypeStruct((ndev, per * nproj, width), BF16),
                jax.ShapeDtypeStruct((per * nproj, width), F32),
            ),
            in_specs=[vmem] * 5,
            out_specs=(vmem, vmem),
            compiler_params=pltpu.CompilerParams(vmem_limit_bytes=24 << 20),
            cost_estimate=pl.CostEstimate(
                flops=6 * nlat * nproj * nchan * width, bytes_accessed=8 << 20, transcendentals=0
            ),
        )(high, low, scaled, last, pooled)
        if index < len(CHUNKS) - 1:
            features, sends = lax.optimization_barrier((features, sends))
        outs += [lax.all_to_all(sends, "tm", 0, 0), own]
        start += width

    latents = pl.pallas_call(
        final_kernel,
        out_shape=jax.ShapeDtypeStruct((per, nproj, npos), F32),
        in_specs=[vmem] * (1 + len(outs)),
        out_specs=vmem,
        compiler_params=pltpu.CompilerParams(vmem_limit_bytes=16 << 20),
        name="final",
    )(counts, *outs)
    return features[None], latents[None]


def solution(mesh):
    return jax.shard_map(
        per_device,
        mesh=mesh,
        in_specs=(P("dp", "tm", None, None), P(None, "dp", None), P(), P(), P("tm"), P("tm"), P()),
        out_specs=(P("dp", "tm", None, None), P("dp", "tm", None, None)),
        check_vma=False,
    )
```

profile of v0, /device:TPU:1, one launch (start us, length us, event | category | flops | bytes accessed | tf_op | source)
XLA Modules:
  0.0 110.5 jit_solution(6721403118021312724)
XLA Ops:
  0.6 1.3 %slice_bitcast_fusion = bf16[2,512,512]{2,1,0:T(8,128)(2,1)S(1)} fusion(bf16[1,16,512,512]{3,2,1,0:T(8,128)(2,1)} %param.7), kind=kLoop, calls=%fused_computation | loop fusion | bytes 2097152 | tf_op jit(solution)/shard_map/slice | solution.py:227
  1.9 4.6 %collective-permute-start = (bf16[2,512,512]{2,1,0:T(8,128)(2,1)S(1)}, bf16[2,512,512]{2,1,0:T(8,128)(2,1)S(1)}, u32[]{:S(2)}, u32[]{:S(2)}) collective-permute-start(bf16[2,512,512]{2,1,0:T(8,128)(2,1)S(1)} %slice_bitcast_fusion), channel_id=1, source_target_pairs={{0,1},{1,2},{2,3},{3,4},{4,5},{5,6},{6,7},{7,8},{8,9},{9,10},{10,1... | collective-permute-start | bytes 3145736 | tf_op jit(solution)/shard_map/ppermute | solution.py:26
  6.5 1.0 broadcast_multiply_fusion.own
  7.6 0.0 copy-start.5
  7.6 2.8 %collective-permute-start.3 = (bf16[3,64,512]{2,1,0:T(8,128)(2,1)S(1)}, bf16[3,64,512]{2,1,0:T(8,128)(2,1)S(1)}, u32[]{:S(2)}, u32[]{:S(2)}) collective-permute-start(bf16[3,64,512]{2,1,0:T(8,128)(2,1)S(1)} %constant_dynamic-slice_fusion), channel_id=1, source_target_pairs={{0,64},{32,96},{64,0},{96,32},{1,65},{33,97},{65,1},{97,33},{2,66}... | collective-permute-start | bytes 589832 | tf_op jit(solution)/shard_map/ppermute | solution.py:21
  10.4 0.9 collective-permute-start.2
  11.3 0.6 collective-permute-start.1
  11.9 1.3 %fusion = (f32[16]{0:T(128)S(1)}, s32[16]{0:T(128)}) fusion(s32[16]{0:T(128)} %param.12, s32[]{:T(128)S(6)} %mul.31), kind=kLoop, calls=%fused_computation.9 | loop fusion | flops 32 | bytes 196 | tf_op jit(solution)/shard_map/convert_element_type | solution.py:232
  13.2 0.7 broadcast_select_fusion
  13.9 0.7 broadcast_in_dim.50
  14.7 7.9 %all-to-all-start = ((f32[32,16,128]{2,1,0:T(8,128)}), f32[32,16,128]{2,1,0:T(8,128)S(1)}, u32[]{:S(2)}, u32[]{:S(2)}) async-start(f32[32,16,128]{2,1,0:T(8,128)} %broadcast_in_dim.50), calls=%async_computation | async-start | bytes 524288 | tf_op jit(solution)/shard_map/all_to_all | solution.py:234
  22.6 1.3 %sqrt_multiply_fusion = (f32[512]{0:T(512)S(1)}, f32[512]{0:T(512)}) fusion(f32[512]{0:T(512)} %param.9, f32[512]{0:T(512)} %param.10), kind=kLoop, calls=%fused_computation.4 | loop fusion | flops 2048 | bytes 8192 | tf_op jit(solution)/shard_map/mul | solution.py:238
  23.9 0.0 collective-permute-done.3.dc
  23.9 0.0 copy-start.7
  23.9 0.2 collective-permute-start.6
  24.1 0.0 collective-permute-done.2.db
  24.1 0.0 copy-start.8
  24.1 0.3 collective-permute-start.5
  24.4 0.0 collective-permute-done.1.da
  24.4 0.2 collective-permute-start.4
  24.6 0.7 multiply_bitcast_fusion.scaled
  25.4 0.0 collective-permute-done.6.sc
  25.4 0.2 collective-permute-done.5.sb
  25.6 0.4 collective-permute-done.4.sa
  26.1 0.0 collective-permute-done.halo_hbm
  26.1 0.0 copy-done.9
  26.1 0.2 copy-done.10
  26.3 0.0 copy-done.5
  26.3 0.0 copy-done.7
  26.3 0.0 copy-done.8
  26.3 0.4 copy-done.11
  26.8 0.4 copy-done.6
  27.1 19.1 %shard_map.86 = (bf16[16,512,512]{2,1,0:T(8,128)(2,1)}, f32[256,512]{1,0:T(8,128)}, f32[3,256,512]{2,1,0:T(8,128)}) custom-call(s32[16]{0:T(128)} %get-tuple-element.39.window, f32[16]{0:T(128)} %keep.3, bf16[16,512,512]{2,1,0:T(8,128)(2,1)} %bitcast.12, bf16[2,512,512]{2,1,0:T(8,128)(2,1)} %copy-done.6, bf16[3,128,512]{2,1,0:T(8,128)(2,1)} %copy-done.5, ...), custom_call_target="tpu_custom_call" | custom-call | flops 6442450944 | bytes 8388608 | tf_op jit(solution)/shard_map/pallas_call | solution.py:276
  46.2 0.0 all-to-all-done
  46.2 0.0 copy-done.4
  46.2 2.8 %tables.1 = (bf16[64,16,512]{2,1,0:T(8,128)(2,1)S(1)}, bf16[64,16,512]{2,1,0:T(8,128)(2,1)S(1)}, f32[2,128]{1,0:T(2,128)S(1)}) custom-call(f32[512,128]{1,0:T(8,128)S(1)} %bitcast.10, f32[1,512]{1,0:T(1,128)S(1)} %bitcast.11, f32[16,512]{1,0:T(8,128)S(1)} %multiply_bitcast_fusion.scaled), custom_call_target="tpu_custom_call" | custom-call | flops 201326592 | bytes 4194304 | tf_op jit(solution)/shard_map/tables/pallas_call | solution.py:279
  49.0 0.0 copy-start.1
  49.0 1.4 %copy-done.1 = f32[3,256,512]{2,1,0:T(8,128)S(1)} copy-done((f32[3,256,512]{2,1,0:T(8,128)S(1)}, f32[3,256,512]{2,1,0:T(8,128)}, u32[]{:S(2)}) %copy-start.1) | copy-done | bytes 1572888
  50.4 1.0 copy-done.3
  51.5 1.5 %shard_map.87 = (bf16[32,32,256]{2,1,0:T(8,128)(2,1)S(1)}, f32[32,256]{1,0:T(8,128)S(1)}) custom-call(bf16[64,16,512]{2,1,0:T(8,128)(2,1)S(1)} %get-tuple-element.22.high, bf16[64,16,512]{2,1,0:T(8,128)(2,1)S(1)} %get-tuple-element.23.low, f32[16,512]{1,0:T(8,128)S(1)} %multiply_bitcast_fusion.scaled, f32[256,512]{1,0:T(8,128)S(1)} %copy-done.3, ...), custom_call_target="tpu_custom_call" | custom-call | flops 805306368 | bytes 8388608 | tf_op jit(solution)/shard_map/pallas_call | solution.py:291
  53.0 19.0 %shard_map.88 = (bf16[16,512,512]{2,1,0:T(8,128)(2,1)}, f32[256,512]{1,0:T(8,128)}, f32[3,256,512]{2,1,0:T(8,128)}) custom-call(s32[16]{0:T(128)} %get-tuple-element.39.window, f32[16]{0:T(128)} %keep.3, bf16[16,512,512]{2,1,0:T(8,128)(2,1)} %bitcast.13, bf16[2,512,512]{2,1,0:T(8,128)(2,1)} %copy-done.6, ...), custom_call_target="tpu_custom_call", output_to_operand_aliasing={{0}: (12, {})} | custom-call | flops 6442450944 | bytes 8388608 | tf_op jit(solution)/shard_map/pallas_call | solution.py:276
  72.0 0.0 copy-start
  72.0 1.4 %copy-done = f32[3,256,512]{2,1,0:T(8,128)S(1)} copy-done((f32[3,256,512]{2,1,0:T(8,128)S(1)}, f32[3,256,512]{2,1,0:T(8,128)}, u32[]{:S(2)}) %copy-start) | copy-done | bytes 1572888
  73.4 1.0 copy-done.2
  74.5 1.5 %shard_map.89 = (bf16[32,32,256]{2,1,0:T(8,128)(2,1)S(1)}, f32[32,256]{1,0:T(8,128)S(1)}) custom-call(bf16[64,16,512]{2,1,0:T(8,128)(2,1)S(1)} %get-tuple-element.22.high, bf16[64,16,512]{2,1,0:T(8,128)(2,1)S(1)} %get-tuple-element.23.low, f32[16,512]{1,0:T(8,128)S(1)} %multiply_bitcast_fusion.scaled, f32[256,512]{1,0:T(8,128)S(1)} %copy-done.2, ...), custom_call_target="tpu_custom_call" | custom-call | flops 805306368 | bytes 8388608 | tf_op jit(solution)/shard_map/pallas_call | solution.py:291
  76.0 18.6 %all_to_all.15.refs_2_ = bf16[32,32,256]{2,1,0:T(8,128)(2,1)S(1)} all-to-all(bf16[32,32,256]{2,1,0:T(8,128)(2,1)S(1)} %get-tuple-element.34), channel_id=1, replica_groups=mesh['dp'=4,'tm'=32] {'tm'}, dimensions={0} | all-to-all | bytes 1048576 | tf_op jit(solution)/shard_map/all_to_all | solution.py:306
  94.6 15.0 %all_to_all.16.refs_0_ = bf16[32,32,256]{2,1,0:T(8,128)(2,1)S(1)} all-to-all(bf16[32,32,256]{2,1,0:T(8,128)(2,1)S(1)} %get-tuple-element.30), channel_id=1, replica_groups=mesh['dp'=4,'tm'=32] {'tm'}, dimensions={0} | all-to-all | bytes 1048576 | tf_op jit(solution)/shard_map/all_to_all | solution.py:306
  109.7 0.8 final.1
  (9 shorter events, 0.0 us)
Async XLA Ops:
  1.9 24.1 %collective-permute-start = (bf16[2,512,512]{2,1,0:T(8,128)(2,1)S(1)}, bf16[2,512,512]{2,1,0:T(8,128)(2,1)S(1)}, u32[]{:S(2)}, u32[]{:S(2)}) collective-permute-start(bf16[2,512,512]{2,1,0:T(8,128)(2,1)S(1)} %slice_bitcast_fusion), channel_id=1, source_target_pairs={{0,1},{1,2},{2,3},{3,4},{4,5},{5,6},{6,7},{7,8},{8,9},{9,10},{10,1... | collective-permute-start | bytes 3145736 | tf_op jit(solution)/shard_map/ppermute | solution.py:26
  7.6 18.7 %copy-start.5 = (bf16[3,128,512]{2,1,0:T(8,128)(2,1)}, bf16[3,128,512]{2,1,0:T(8,128)(2,1)S(1)}, u32[]{:S(2)}) copy-start(bf16[3,128,512]{2,1,0:T(8,128)(2,1)S(1)} %broadcast_multiply_fusion.own) | copy-start | bytes 1179652
  7.6 16.3 %collective-permute-start.3 = (bf16[3,64,512]{2,1,0:T(8,128)(2,1)S(1)}, bf16[3,64,512]{2,1,0:T(8,128)(2,1)S(1)}, u32[]{:S(2)}, u32[]{:S(2)}) collective-permute-start(bf16[3,64,512]{2,1,0:T(8,128)(2,1)S(1)} %constant_dynamic-slice_fusion), channel_id=1, source_target_pairs={{0,64},{32,96},{64,0},{96,32},{1,65},{33,97},{65,1},{97,33},{2,66}... | collective-permute-start | bytes 589832 | tf_op jit(solution)/shard_map/ppermute | solution.py:21
  10.4 13.7 %collective-permute-start.2 = (bf16[3,64,512]{2,1,0:T(8,128)(2,1)S(1)}, bf16[3,64,512]{2,1,0:T(8,128)(2,1)S(1)}, u32[]{:S(2)}, u32[]{:S(2)}) collective-permute-start(bf16[3,64,512]{2,1,0:T(8,128)(2,1)S(1)} %constant_dynamic-slice_fusion), channel_id=1, source_target_pairs={{0,96},{32,0},{64,32},{96,64},{1,97},{33,1},{65,33},{97,65},{2,98}... | collective-permute-start | bytes 589832 | tf_op jit(solution)/shard_map/ppermute | solution.py:21
  11.3 13.1 %collective-permute-start.1 = (bf16[3,64,512]{2,1,0:T(8,128)(2,1)S(1)}, bf16[3,64,512]{2,1,0:T(8,128)(2,1)}, u32[]{:S(2)}, u32[]{:S(2)}) collective-permute-start(bf16[3,64,512]{2,1,0:T(8,128)(2,1)S(1)} %constant_dynamic-slice_fusion), channel_id=1, source_target_pairs={{0,32},{32,64},{64,96},{96,0},{1,33},{33,65},{65,97},{97,1},{2,34}... | collective-permute-start | bytes 589832 | tf_op jit(solution)/shard_map/ppermute | solution.py:21
  14.7 31.6 %all-to-all-start = ((f32[32,16,128]{2,1,0:T(8,128)}), f32[32,16,128]{2,1,0:T(8,128)S(1)}, u32[]{:S(2)}, u32[]{:S(2)}) async-start(f32[32,16,128]{2,1,0:T(8,128)} %broadcast_in_dim.50), calls=%async_computation | async-start | bytes 524288 | tf_op jit(solution)/shard_map/all_to_all | solution.py:234
  23.9 2.4 %copy-start.7 = (bf16[3,64,512]{2,1,0:T(8,128)(2,1)}, bf16[3,64,512]{2,1,0:T(8,128)(2,1)S(1)}, u32[]{:S(2)}) copy-start(bf16[3,64,512]{2,1,0:T(8,128)(2,1)S(1)} %collective-permute-done.3.dc) | copy-start | bytes 589828
  23.9 1.5 %collective-permute-start.6 = (bf16[3,64,512]{2,1,0:T(8,128)(2,1)S(1)}, bf16[3,64,512]{2,1,0:T(8,128)(2,1)S(1)}, u32[]{:S(2)}, u32[]{:S(2)}) collective-permute-start(bf16[3,64,512]{2,1,0:T(8,128)(2,1)S(1)} %collective-permute-done.3.dc), channel_id=1, source_target_pairs={{0,1},{1,0},{2,3},{3,2},{4,5},{5,4},{6,7},{7,6},{8,9},{9,8},{10,11... | collective-permute-start | bytes 589832 | tf_op jit(solution)/shard_map/ppermute | solution.py:30
  24.1 2.2 %copy-start.8 = (bf16[3,64,512]{2,1,0:T(8,128)(2,1)}, bf16[3,64,512]{2,1,0:T(8,128)(2,1)S(1)}, u32[]{:S(2)}) copy-start(bf16[3,64,512]{2,1,0:T(8,128)(2,1)S(1)} %collective-permute-done.2.db) | copy-start | bytes 589828
  24.1 1.5 %collective-permute-start.5 = (bf16[3,64,512]{2,1,0:T(8,128)(2,1)S(1)}, bf16[3,64,512]{2,1,0:T(8,128)(2,1)S(1)}, u32[]{:S(2)}, u32[]{:S(2)}) collective-permute-start(bf16[3,64,512]{2,1,0:T(8,128)(2,1)S(1)} %collective-permute-done.2.db), channel_id=1, source_target_pairs={{0,1},{1,0},{2,3},{3,2},{4,5},{5,4},{6,7},{7,6},{8,9},{9,8},{10,11... | collective-permute-start | bytes 589832 | tf_op jit(solution)/shard_map/ppermute | solution.py:30
  24.4 1.7 %collective-permute-start.4 = (bf16[3,64,512]{2,1,0:T(8,128)(2,1)}, bf16[3,64,512]{2,1,0:T(8,128)(2,1)S(1)}, u32[]{:S(2)}, u32[]{:S(2)}) collective-permute-start(bf16[3,64,512]{2,1,0:T(8,128)(2,1)} %collective-permute-done.1.da), channel_id=1, source_target_pairs={{0,1},{1,0},{2,3},{3,2},{4,5},{5,4},{6,7},{7,6},{8,9},{9,8},{10,11... | collective-permute-start | bytes 589832 | tf_op jit(solution)/shard_map/ppermute | solution.py:30
  25.4 0.7 copy-start.9
  25.6 0.7 copy-start.10
  26.1 0.7 copy-start.11
  26.1 1.0 copy-start.6
  27.1 19.1 %copy-start.4 = (f32[512]{0:T(512)S(1)}, f32[512]{0:T(512)}, u32[]{:S(2)}) copy-start(f32[512]{0:T(512)} %param.10) | copy-start | bytes 6148
  49.0 1.4 %copy-start.1 = (f32[3,256,512]{2,1,0:T(8,128)S(1)}, f32[3,256,512]{2,1,0:T(8,128)}, u32[]{:S(2)}) copy-start(f32[3,256,512]{2,1,0:T(8,128)} %get-tuple-element.25.pooled) | copy-start | bytes 4718596
  50.4 1.0 copy-start.3
  72.0 1.4 %copy-start = (f32[3,256,512]{2,1,0:T(8,128)S(1)}, f32[3,256,512]{2,1,0:T(8,128)}, u32[]{:S(2)}) copy-start(f32[3,256,512]{2,1,0:T(8,128)} %get-tuple-element.33.pooled) | copy-start | bytes 4718596
  73.4 1.0 copy-start.2
where the time goes:
time: 111 us; the launch traced here: 110 us
  Pallas kernels  44.7 us (40%)
  blocking collectives  33.7 us (30%)
  starting transfers between devices  17.5 us (16%)
  local copies, waits for them, and re-layouts  7.98 us (7%)
  other arithmetic  5.08 us (5%)
    pallas_call x2, Pallas kernels, per_device(): conv(window, keep, x, halo, own_w, da, db, dc, sa, sb, sc, decay, *before)  38.1 us
    all_to_all x2, blocking collectives, per_device(): outs += [lax.all_to_all(sends, 'tm', 0, 0), own]  33.7 us
    all_to_all x1, starting transfers between devices, per_device(): packed = lax.all_to_all(local, 'tm', 0, 0).reshape(nall, 128)  7.92 us
    unnamed x24, local copies, waits for them, and re-layouts  5.94 us
    ppermute x1, starting transfers between devices, shifted(): lax.ppermute(value, axis, [(s, s + steps) for s in range(count - steps)])  4.58 us
    ppermute x3, starting transfers between devices, rotated(): lax.ppermute(value, axis, [(s, (s + steps) % count) for s in range(count)])  4.29 us
    pallas_call x2, Pallas kernels, per_device(): pl.pallas_call(spread_kernel, out_shape=(jax.ShapeDtypeStruct((ndev, per...  3.07 us
    pallas_call x1, Pallas kernels, per_device(): pl.pallas_call(table_kernel, out_shape=(table_shape, table_shape, jax.Sha...  2.77 us
  transfers between devices with their start and end apart: 8, of which 2 were waited for; matrix products, arithmetic and copies ran while one was open for 5% of the time, Pallas kernels for 17%

commit v1 on v0

v1 whole, which is shorter than its diff:
```python
import functools

import jax
import jax.numpy as jnp
from jax import lax
from jax.experimental import pallas as pl
from jax.experimental.pallas import tpu as pltpu
from jax.sharding import PartitionSpec as P


KT = 3
STRIDE = 8
F32 = jnp.float32
BF16 = jnp.bfloat16
TILE = 128
GROUP = 4
ROWS = 256
SUB = 16


def rotated(value, axis, steps):
    count = lax.axis_size(axis)
    return lax.ppermute(value, axis, [(s, (s + steps) % count) for s in range(count)])


def shifted(value, axis, steps):
    count = lax.axis_size(axis)
    return lax.ppermute(value, axis, [(s, s + steps) for s in range(count - steps)])


def swapped(value, axis):
    return lax.ppermute(value, axis, [(s, s ^ 1) for s in range(lax.axis_size(axis))])


def table_kernel(packed, rate, scaled, high, low, counts, E):
    nall, lanes = packed.shape
    nchan = rate.shape[1]
    nlat = high.shape[0]
    me = lax.axis_index("tm")
    end = (me + 1) * (nall // lax.axis_size("tm")) - 1
    frame = lax.broadcasted_iota(jnp.int32, (nall, lanes), 0)
    logs = jnp.where(frame > end, jnp.log(jnp.maximum(packed[...], 0.5)), 0.0)
    rows = lax.broadcasted_iota(jnp.int32, (nall, nall), 0)
    cols = lax.broadcasted_iota(jnp.int32, (nall, nall), 1)
    run = jnp.dot(
        (cols <= rows).astype(F32), logs, precision=lax.Precision.HIGHEST, preferred_element_type=F32
    )
    block = 128
    for r in range(0, nall, block):
        at = lax.broadcasted_iota(jnp.int32, (block, nchan), 0) + r
        gap = (at - end).astype(F32)
        E[r : r + block, :] = jnp.where(at > end, jnp.exp(run[r : r + block, 0:1] - rate[...] * gap), 0.0)
    ids = packed[:, lanes // 2 : lanes // 2 + 1].astype(jnp.int32)
    member = (lax.broadcasted_iota(jnp.int32, (nall, lanes), 1) == ids).astype(F32)
    table = lax.dot_general(
        member, E[...], (((0,), (0,)), ((), ())), precision=lax.Precision.HIGHEST, preferred_element_type=F32
    )
    per = counts.shape[0]
    for i in range(per):
        hit = (jnp.broadcast_to(ids, (nall, lanes)) == me * per + i).astype(F32)
        counts[i : i + 1, :] = jnp.sum(hit, 0, keepdims=True)
    E[0:lanes, :] = table
    for j in range(nlat):
        value = scaled[...] * E[j : j + 1, :]
        upper = value.astype(BF16)
        high[j] = upper
        low[j] = (value - upper.astype(F32)).astype(BF16)


def times(a, b):
    return lax.dot_general(a, b, (((1,), (1,)), ((), ())), preferred_element_type=F32)


def split(value):
    upper = value.astype(BF16)
    return upper, (value - upper.astype(F32)).astype(BF16)


def spread(high, low, scaled, last, pooled, sends, own):
    nlat, nproj, nchan = high.shape
    ndev = sends.shape[0]
    width = last.shape[0]
    top, rest = split(last[...])
    rows = 256
    per = sends.shape[1]
    for r in range(0, nlat * nproj, rows):
        upper = high[r // nproj : (r + rows) // nproj].reshape(rows, nchan)
        lower = low[r // nproj : (r + rows) // nproj].reshape(rows, nchan)
        z = times(upper, top) + times(upper, rest) + times(lower, top)
        sends[r // per : (r + rows) // per] = z.reshape(rows // per, per, width).astype(BF16)
    upper, lower = split(scaled[...])
    parts = []
    for j in range(3):
        top, rest = split(pooled[j])
        parts.append(times(upper, top) + times(upper, rest) + times(lower, top))
    own[0:nproj, :] = parts[0]
    own[nproj : 2 * nproj, :] = parts[1]
    me = lax.axis_index("tm")

    @pl.when(me < ndev - 1)
    def _():
        block = sends[me + 1]
        sends[me + 1, 0:nproj] = (block[0:nproj].astype(F32) + parts[2]).astype(BF16)


def conv_kernel(
    window, keep, x_hbm, halo_hbm, own_w, da, db, dc, sa, sb, sc, decay, high, low, scaled,
    feat_hbm, sends, own, w, X, HA, HB, FA, FB, R, last, pooled, wsem, insem, outsem, *, shards,
):
    nframe, npos, nchan = x_hbm.shape
    tiles, groups = npos // TILE, nframe // GROUP
    total = tiles * groups
    H, F = (HA, HB), (FA, FB)
    half, depth = da.shape[1], own_w.shape[1]
    me = lax.axis_index("dp")
    side = lax.rem(lax.axis_index("tm"), 2)
    lead = KT - 1

    def weights():
        copies = [pltpu.make_async_copy(own_w, w.at[:, pl.ds(pl.multiple_of(me * depth, depth), depth)], wsem.at[0])]
        slot = 1
        for step, mine, other in ((shards - 1, da, sa), (1, db, sb), (2, dc, sc)):
            base = lax.rem(me + step, shards) * depth
            for piece, lane in ((mine, side), (other, 1 - side)):
                row = pl.multiple_of(base + lane * half, half)
                copies.append(pltpu.make_async_copy(piece, w.at[:, pl.ds(row, half)], wsem.at[slot]))
                slot += 1
        return copies

    def entering(q):
        part = pl.ds(q * TILE, TILE)
        return pltpu.make_async_copy(x_hbm.at[:, part], X.at[lead : lead + nframe, part], insem.at[q])

    def prior(q):
        part = pl.ds(q * TILE, TILE)
        return pltpu.make_async_copy(halo_hbm.at[:, part], X.at[0:lead, part], insem.at[tiles + q])

    def place(i):
        return pl.multiple_of(i // groups * TILE, TILE), lax.rem(i, groups) * GROUP

    def leaving(i, s):
        p, f = place(i)
        return pltpu.make_async_copy(F[s], feat_hbm.at[pl.ds(f, GROUP), pl.ds(p, TILE)], outsem.at[s])

    def product(i, s, m, n):
        p, f = place(i)
        count = ROWS // TILE
        acc = None
        for k in range(KT):
            rows = X[pl.ds(f + lead - k + m * count, count), pl.ds(p, TILE), :].reshape(ROWS, nchan)
            part = jnp.dot(rows, w[k, :, n : n + 256], preferred_element_type=F32)
            acc = part if acc is None else acc + part
        H[s][m * ROWS : (m + 1) * ROWS, n : n + 256] = acc

    def activate(i, s, g, r):
        p, f = place(i)
        at = g * TILE + r
        h = H[s][at : at + SUB, :]
        c = X[f + lead + g, pl.ds(p + r, SUB), :].astype(F32)
        value = c + (h + h * jnp.tanh(h))
        F[s][g, r : r + SUB, :] = value.astype(BF16)
        mean = jnp.sum(value * value, -1, keepdims=True) * (1.0 / nchan)
        R[at : at + SUB, :] = jnp.broadcast_to(lax.rsqrt(mean + 1e-06), (SUB, 128))

    def recur(i, s, r):
        p, f = place(i)
        rows = pl.ds(p + r, SUB)
        state = last[rows, :]
        for g in range(GROUP):
            scale = R[g * TILE + r : g * TILE + r + SUB, :]
            v = F[s][g, r : r + SUB, :].astype(F32)
            v = jnp.concatenate([v[:, n : n + 128] * scale for n in range(0, nchan, 128)], 1)
            state = state * (decay[...] * keep[f + g]) + v
            pooled[window[f + g], rows, :] += state
        last[rows, :] = state

    products = [(m, n) for m in range(GROUP * TILE // ROWS) for n in range(0, nchan, 256)]

    def stage(later, ls, i, s):
        work = [(g, r) for r in range(0, TILE, SUB) for g in range(GROUP)] + [(None, r) for r in range(0, TILE, SUB)]
        todo = list(products)
        for at, (g, r) in enumerate(work):
            if todo and at * len(products) // len(work) >= len(products) - len(todo):
                product(later, ls, *todo.pop(0))
            if g is None:
                recur(i, s, r)
            else:
                activate(i, s, g, r)

    pieces = weights()
    for copy in pieces:
        copy.start()
    for q in range(tiles):
        prior(q).start()
        entering(q).start()
    last[...] = jnp.zeros_like(last)
    pooled[...] = jnp.zeros_like(pooled)
    for copy in pieces:
        copy.wait()
    prior(0).wait()
    entering(0).wait()
    for m, n in products:
        product(0, 0, m, n)

    def body(step, _):
        i = 2 * step

        @pl.when(step > 0)
        def _():
            leaving(i - 2, 0).wait()
            leaving(i - 1, 1).wait()

        stage(i + 1, 1, i, 0)
        leaving(i, 0).start()
        q = (i + 2) // groups

        @pl.when(jnp.logical_and(lax.rem(i + 2, groups) == 0, q < tiles))
        def _():
            prior(q).wait()
            entering(q).wait()

        stage(lax.rem(i + 2, total), 0, i + 1, 1)
        leaving(i + 1, 1).start()
        return 0

    lax.fori_loop(0, total // 2, body, 0)
    spread(high, low, scaled, last, pooled, sends, own)
    leaving(total - 2, 0).wait()
    leaving(total - 1, 1).wait()


def final_kernel(counts, *refs):
    per = counts.shape[0]
    latents = refs[-1]
    start = 0
    for index in range(len(refs) // 2):
        got, own = refs[2 * index], refs[2 * index + 1]
        ndev, rows, width = got.shape
        nproj = rows // per
        for i in range(per):
            part = slice(i * nproj, (i + 1) * nproj)
            total = own[part, :]
            for d in range(ndev):
                total = total + got[d, part, :].astype(F32)
            for n in range(0, width, 128):
                latents[i, :, start + n : start + n + 128] = total[:, n : n + 128] / counts[i : i + 1, :]
        start += width


def per_device(clips, w_time, gain, rate, keep, latent_ids, w_lat):
    _, nframe, npos, nchan = clips.shape
    nproj = w_lat.shape[1]
    ndev = lax.axis_size("tm")
    shards = lax.axis_size("dp")
    nall = nframe * ndev
    per = nframe // STRIDE
    nlat = per * ndev
    me = lax.axis_index("tm")
    side = me % 2
    x = clips[0]

    own_w = w_time * jnp.asarray(0.5, BF16)
    half = own_w.shape[1] // 2
    mine = lax.dynamic_slice_in_dim(own_w, side * half, half, 1)
    dc, da, db = rotated(mine, "dp", 2), rotated(mine, "dp", 1), rotated(mine, "dp", -1)
    sa, sb, sc = swapped(da, "tm"), swapped(db, "tm"), swapped(dc, "tm")
    source, keep, latent_ids, rate, gain, w_lat, _ = lax.optimization_barrier(
        (x, keep, latent_ids, rate, gain, w_lat, mine)
    )
    halo = shifted(source[nframe - (KT - 1) :], "tm", 1)
    lane = jnp.arange(128, dtype=jnp.int32)[None]
    local = jnp.where(lane < 64, keep[:, None], latent_ids.astype(F32)[:, None])
    local = jnp.broadcast_to(local[None], (ndev, nframe, 128))
    packed = lax.all_to_all(local, "tm", 0, 0).reshape(nall, 128)

    decay = jnp.exp(-rate)[None]
    inject = jnp.sqrt(-jnp.expm1(-2.0 * rate))
    scaled = w_lat.T.astype(F32) * (inject * gain)[None]

    vmem = pl.BlockSpec(memory_space=pltpu.VMEM)
    smem = pl.BlockSpec(memory_space=pltpu.SMEM)
    hbm = pl.BlockSpec(memory_space=pltpu.HBM)
    table_shape = jax.ShapeDtypeStruct((nlat, nproj, nchan), BF16)

    window = latent_ids - me.astype(jnp.int32) * per
    high, low, counts = pl.pallas_call(
        table_kernel,
        out_shape=(table_shape, table_shape, jax.ShapeDtypeStruct((per, 128), F32)),
        in_specs=[vmem] * 3,
        out_specs=(vmem,) * 3,
        scratch_shapes=[pltpu.VMEM((nall, nchan), F32)],
        compiler_params=pltpu.CompilerParams(vmem_limit_bytes=24 << 20),
        cost_estimate=pl.CostEstimate(
            flops=12 * nlat * nall * nchan, bytes_accessed=4 << 20, transcendentals=nall * nchan
        ),
        name="tables",
    )(packed, rate[None], scaled)
    stage_rows = GROUP * TILE
    features, sends, own = pl.pallas_call(
        functools.partial(conv_kernel, shards=shards),
        out_shape=(
            jax.ShapeDtypeStruct((nframe, npos, nchan), BF16),
            jax.ShapeDtypeStruct((ndev, per * nproj, npos), BF16),
            jax.ShapeDtypeStruct((per * nproj, npos), F32),
        ),
        in_specs=[smem, smem] + [hbm] * 9 + [vmem] * 4,
        out_specs=(hbm, vmem, vmem),
        scratch_shapes=[
            pltpu.VMEM((KT, nchan, nchan), BF16),
            pltpu.VMEM((nframe + KT - 1, npos, nchan), BF16),
            pltpu.VMEM((stage_rows, nchan), F32),
            pltpu.VMEM((stage_rows, nchan), F32),
            pltpu.VMEM((GROUP, TILE, nchan), BF16),
            pltpu.VMEM((GROUP, TILE, nchan), BF16),
            pltpu.VMEM((stage_rows, 128), F32),
            pltpu.VMEM((npos, nchan), F32),
            pltpu.VMEM((3, npos, nchan), F32),
            pltpu.SemaphoreType.DMA((7,)),
            pltpu.SemaphoreType.DMA((2 * npos // TILE,)),
            pltpu.SemaphoreType.DMA((2,)),
        ],
        compiler_params=pltpu.CompilerParams(vmem_limit_bytes=44 << 20),
        cost_estimate=pl.CostEstimate(
            flops=2 * KT * nframe * npos * nchan * nchan,
            bytes_accessed=4 * nframe * npos * nchan,
            transcendentals=nframe * npos * nchan,
        ),
        name="conv",
    )(window, keep, x, halo, own_w, da, db, dc, sa, sb, sc, decay, high, low, scaled)
    outs = [lax.all_to_all(sends, "tm", 0, 0), own]
    latents = pl.pallas_call(
        final_kernel,
        out_shape=jax.ShapeDtypeStruct((per, nproj, npos), F32),
        in_specs=[vmem] * (1 + len(outs)),
        out_specs=vmem,
        compiler_params=pltpu.CompilerParams(vmem_limit_bytes=16 << 20),
        name="final",
    )(counts, *outs)
    return features[None], latents[None]


def solution(mesh):
    return jax.shard_map(
        per_device,
        mesh=mesh,
        in_specs=(P("dp", "tm", None, None), P(None, "dp", None), P(), P(), P("tm"), P("tm"), P()),
        out_specs=(P("dp", "tm", None, None), P("dp", "tm", None, None)),
        check_vma=False,
    )
```

time: 111 us -> 88 us (0.79)
  blocking collectives: 33.7 us -> 20.6 us
  Pallas kernels: 44.7 us -> 33.7 us
  waiting for transfers between devices: 0.7 us -> 6.61 us
  local copies, waits for them, and re-layouts: 7.98 us -> 4.34 us
  other arithmetic: 5.08 us -> 3.93 us
    all_to_all x2 -> x1, blocking collectives: 33.7 us -> 20.6 us  [per_device(): outs = [lax.all_to_all(sends, 'tm', 0, 0), own]]
    pallas_call x4 -> x1, Pallas kernels: 41.2 us -> 30.1 us  [per_device(): pl.pallas_call(functools.partial(conv_kernel, shards=shards), out_shape=(...]
    all_to_all x1, waiting for transfers between devices: 0.01 us -> 6.59 us  [per_device(): packed = lax.all_to_all(local, 'tm', 0, 0).reshape(nall, 128)]
    unnamed x24 -> x4, local copies, waits for them, and re-layouts: 5.94 us -> 1.33 us
  transfers between devices with their start and end apart: 8 -> 8, of which waited for: 2 -> 1; matrix products, arithmetic and copies ran while one was open for 5% -> 4% of each run, Pallas kernels for 17% -> 3%
where the time goes in v1:
time: 88 us; the launch traced here: 87.5 us
  Pallas kernels  33.7 us (38%)
  blocking collectives  20.6 us (23%)
  starting transfers between devices  17.6 us (20%)
  waiting for transfers between devices  6.61 us (8%)
  local copies, waits for them, and re-layouts  4.34 us (5%)
  other arithmetic  3.93 us (4%)
    pallas_call x1, Pallas kernels, per_device(): pl.pallas_call(functools.partial(conv_kernel, shards=shards), out_shape=(...  30.1 us
    all_to_all x1, blocking collectives, per_device(): outs = [lax.all_to_all(sends, 'tm', 0, 0), own]  20.6 us
    all_to_all x1, starting transfers between devices, per_device(): packed = lax.all_to_all(local, 'tm', 0, 0).reshape(nall, 128)  7.92 us
    all_to_all x1, waiting for transfers between devices, per_device(): packed = lax.all_to_all(local, 'tm', 0, 0).reshape(nall, 128)  6.59 us
    ppermute x1, starting transfers between devices, shifted(): lax.ppermute(value, axis, [(s, s + steps) for s in range(count - steps)])  4.57 us
    ppermute x3, starting transfers between devices, rotated(): lax.ppermute(value, axis, [(s, (s + steps) % count) for s in range(count)])  4.29 us
    pallas_call x1, Pallas kernels, per_device(): pl.pallas_call(table_kernel, out_shape=(table_shape, table_shape, jax.Sha...  2.77 us
    slice x1, local copies, waits for them, and re-layouts, per_device(): halo = shifted(source[nframe - (KT - 1):], 'tm', 1)  2.27 us
  transfers between devices with their start and end apart: 8, of which 1 were waited for; matrix products, arithmetic and copies ran while one was open for 4% of the time, Pallas kernels for 3%

profile of v1, /device:TPU:1, one launch (start us, length us, event | category | flops | bytes accessed | tf_op | source)
XLA Modules:
  0.0 87.5 jit_solution(13917395707421385100)
XLA Ops:
  0.6 1.0 %broadcast_multiply_fusion.own_w = bf16[3,128,512]{2,1,0:T(8,128)(2,1)S(1)} fusion(bf16[3,128,512]{2,1,0:T(8,128)(2,1)} %param.8), kind=kLoop, calls=%fused_computation | loop fusion | flops 196608 | bytes 786432 | tf_op jit(solution)/shard_map/mul | solution.py:262
  1.7 2.3 %slice.3 = bf16[2,512,512]{2,1,0:T(8,128)(2,1)} slice(bf16[16,512,512]{2,1,0:T(8,128)(2,1)} %bitcast.11), slice={[14:16], [0:512], [0:512]} | slice | bytes 2097152 | tf_op jit(solution)/shard_map/slice | solution.py:270
  4.0 4.6 %collective-permute-start = (bf16[2,512,512]{2,1,0:T(8,128)(2,1)}, bf16[2,512,512]{2,1,0:T(8,128)(2,1)S(1)}, u32[]{:S(2)}, u32[]{:S(2)}) collective-permute-start(bf16[2,512,512]{2,1,0:T(8,128)(2,1)} %slice.3), channel_id=1, source_target_pairs={{0,1},{1,2},{2,3},{3,4},{4,5},{5,6},{6,7},{7,8},{8,9},{9,10},{10,1... | collective-permute-start | bytes 3145736 | tf_op jit(solution)/shard_map/ppermute | solution.py:28
  8.6 2.8 %collective-permute-start.3 = (bf16[3,64,512]{2,1,0:T(8,128)(2,1)S(1)}, bf16[3,64,512]{2,1,0:T(8,128)(2,1)S(1)}, u32[]{:S(2)}, u32[]{:S(2)}) collective-permute-start(bf16[3,64,512]{2,1,0:T(8,128)(2,1)S(1)} %constant_dynamic-slice_fusion), channel_id=1, source_target_pairs={{0,64},{32,96},{64,0},{96,32},{1,65},{33,97},{65,1},{97,33},{2,66}... | collective-permute-start | bytes 589832 | tf_op jit(solution)/shard_map/ppermute | solution.py:23
  11.4 0.9 collective-permute-start.2
  12.2 0.6 collective-permute-start.1
  12.9 0.7 fusion
  13.6 0.7 broadcast_select_fusion
  14.3 0.7 broadcast_in_dim.50
  15.0 7.9 %all-to-all-start = ((f32[32,16,128]{2,1,0:T(8,128)}), f32[32,16,128]{2,1,0:T(8,128)S(1)}, u32[]{:S(2)}, u32[]{:S(2)}) async-start(f32[32,16,128]{2,1,0:T(8,128)} %broadcast_in_dim.50), calls=%async_computation | async-start | bytes 524288 | tf_op jit(solution)/shard_map/all_to_all | solution.py:274
  23.0 0.7 sqrt_multiply_fusion
  23.7 0.0 collective-permute-done.3.dc
  23.7 0.3 collective-permute-start.6
  24.0 0.0 collective-permute-done.2.db
  24.0 0.3 collective-permute-start.5
  24.3 0.0 collective-permute-done.1.da
  24.3 0.2 collective-permute-start.4
  24.5 0.7 multiply_bitcast_fusion.scaled
  25.2 6.6 %all-to-all-done = f32[32,16,128]{2,1,0:T(8,128)S(1)} async-done(((f32[32,16,128]{2,1,0:T(8,128)}), f32[32,16,128]{2,1,0:T(8,128)S(1)}, u32[]{:S(2)}, u32[]{:S(2)}) %all-to-all-start) | async-done | bytes 262176 | tf_op jit(solution)/shard_map/all_to_all | solution.py:274
  31.8 0.0 copy-start
  31.8 0.7 copy-done
  32.5 2.8 %tables.1 = (bf16[64,16,512]{2,1,0:T(8,128)(2,1)S(1)}, bf16[64,16,512]{2,1,0:T(8,128)(2,1)S(1)}, f32[2,128]{1,0:T(2,128)S(1)}) custom-call(f32[512,128]{1,0:T(8,128)S(1)} %bitcast.8, f32[1,512]{1,0:T(1,128)S(1)} %bitcast.9, f32[16,512]{1,0:T(8,128)S(1)} %multiply_bitcast_fusion.scaled), custom_call_target="tpu_custom_call" | custom-call | flops 201326592 | bytes 4194304 | tf_op jit(solution)/shard_map/tables/pallas_call | solution.py:286
  35.3 0.0 collective-permute-done.6.sc
  35.3 0.0 collective-permute-done.5.sb
  35.3 0.0 collective-permute-done.4.sa
  35.3 0.0 collective-permute-done.halo_hbm
  35.3 0.0 copy-start.1
  35.4 0.6 copy-done.1
  36.0 30.1 %conv.1 = (bf16[16,512,512]{2,1,0:T(8,128)(2,1)}, bf16[32,32,512]{2,1,0:T(8,128)(2,1)S(1)}, f32[32,512]{1,0:T(8,128)S(1)}) custom-call(s32[16]{0:T(128)S(1)} %get-tuple-element.29.window, f32[16]{0:T(128)S(1)} %copy-done.1, bf16[16,512,512]{2,1,0:T(8,128)(2,1)} %bitcast.12, bf16[2,512,512]{2,1,0:T(8,128)(2,1)S(1)} %collective-permute-done.halo_hbm, ...), custom_call_target="tpu_custom_call" | custom-call | flops 12884901888 | bytes 16777216 | tf_op jit(solution)/shard_map/conv/pallas_call | solution.py:299
  66.1 20.6 %all_to_all.10.refs_0_ = bf16[32,32,512]{2,1,0:T(8,128)(2,1)S(1)} all-to-all(bf16[32,32,512]{2,1,0:T(8,128)(2,1)S(1)} %get-tuple-element.24), channel_id=1, replica_groups=mesh['dp'=4,'tm'=32] {'tm'}, dimensions={0} | all-to-all | bytes 2097152 | tf_op jit(solution)/shard_map/all_to_all | solution.py:330
  86.7 0.8 final.1
  (2 shorter events, 0.0 us)
Async XLA Ops:
  4.0 31.4 %collective-permute-start = (bf16[2,512,512]{2,1,0:T(8,128)(2,1)}, bf16[2,512,512]{2,1,0:T(8,128)(2,1)S(1)}, u32[]{:S(2)}, u32[]{:S(2)}) collective-permute-start(bf16[2,512,512]{2,1,0:T(8,128)(2,1)} %slice.3), channel_id=1, source_target_pairs={{0,1},{1,2},{2,3},{3,4},{4,5},{5,6},{6,7},{7,8},{8,9},{9,10},{10,1... | collective-permute-start | bytes 3145736 | tf_op jit(solution)/shard_map/ppermute | solution.py:28
  8.6 15.1 %collective-permute-start.3 = (bf16[3,64,512]{2,1,0:T(8,128)(2,1)S(1)}, bf16[3,64,512]{2,1,0:T(8,128)(2,1)S(1)}, u32[]{:S(2)}, u32[]{:S(2)}) collective-permute-start(bf16[3,64,512]{2,1,0:T(8,128)(2,1)S(1)} %constant_dynamic-slice_fusion), channel_id=1, source_target_pairs={{0,64},{32,96},{64,0},{96,32},{1,65},{33,97},{65,1},{97,33},{2,66}... | collective-permute-start | bytes 589832 | tf_op jit(solution)/shard_map/ppermute | solution.py:23
  11.4 12.6 %collective-permute-start.2 = (bf16[3,64,512]{2,1,0:T(8,128)(2,1)S(1)}, bf16[3,64,512]{2,1,0:T(8,128)(2,1)S(1)}, u32[]{:S(2)}, u32[]{:S(2)}) collective-permute-start(bf16[3,64,512]{2,1,0:T(8,128)(2,1)S(1)} %constant_dynamic-slice_fusion), channel_id=1, source_target_pairs={{0,96},{32,0},{64,32},{96,64},{1,97},{33,1},{65,33},{97,65},{2,98}... | collective-permute-start | bytes 589832 | tf_op jit(solution)/shard_map/ppermute | solution.py:23
  12.2 12.0 %collective-permute-start.1 = (bf16[3,64,512]{2,1,0:T(8,128)(2,1)S(1)}, bf16[3,64,512]{2,1,0:T(8,128)(2,1)S(1)}, u32[]{:S(2)}, u32[]{:S(2)}) collective-permute-start(bf16[3,64,512]{2,1,0:T(8,128)(2,1)S(1)} %constant_dynamic-slice_fusion), channel_id=1, source_target_pairs={{0,32},{32,64},{64,96},{96,0},{1,33},{33,65},{65,97},{97,1},{2,34}... | collective-permute-start | bytes 589832 | tf_op jit(solution)/shard_map/ppermute | solution.py:23
  15.0 16.8 %all-to-all-start = ((f32[32,16,128]{2,1,0:T(8,128)}), f32[32,16,128]{2,1,0:T(8,128)S(1)}, u32[]{:S(2)}, u32[]{:S(2)}) async-start(f32[32,16,128]{2,1,0:T(8,128)} %broadcast_in_dim.50), calls=%async_computation | async-start | bytes 524288 | tf_op jit(solution)/shard_map/all_to_all | solution.py:274
  23.7 11.6 %collective-permute-start.6 = (bf16[3,64,512]{2,1,0:T(8,128)(2,1)S(1)}, bf16[3,64,512]{2,1,0:T(8,128)(2,1)S(1)}, u32[]{:S(2)}, u32[]{:S(2)}) collective-permute-start(bf16[3,64,512]{2,1,0:T(8,128)(2,1)S(1)} %collective-permute-done.3.dc), channel_id=1, source_target_pairs={{0,1},{1,0},{2,3},{3,2},{4,5},{5,4},{6,7},{7,6},{8,9},{9,8},{10,11... | collective-permute-start | bytes 589832 | tf_op jit(solution)/shard_map/ppermute | solution.py:32
  24.0 11.3 %collective-permute-start.5 = (bf16[3,64,512]{2,1,0:T(8,128)(2,1)S(1)}, bf16[3,64,512]{2,1,0:T(8,128)(2,1)S(1)}, u32[]{:S(2)}, u32[]{:S(2)}) collective-permute-start(bf16[3,64,512]{2,1,0:T(8,128)(2,1)S(1)} %collective-permute-done.2.db), channel_id=1, source_target_pairs={{0,1},{1,0},{2,3},{3,2},{4,5},{5,4},{6,7},{7,6},{8,9},{9,8},{10,11... | collective-permute-start | bytes 589832 | tf_op jit(solution)/shard_map/ppermute | solution.py:32
  24.3 11.0 %collective-permute-start.4 = (bf16[3,64,512]{2,1,0:T(8,128)(2,1)S(1)}, bf16[3,64,512]{2,1,0:T(8,128)(2,1)S(1)}, u32[]{:S(2)}, u32[]{:S(2)}) collective-permute-start(bf16[3,64,512]{2,1,0:T(8,128)(2,1)S(1)} %collective-permute-done.1.da), channel_id=1, source_target_pairs={{0,1},{1,0},{2,3},{3,2},{4,5},{5,4},{6,7},{7,6},{8,9},{9,8},{10,11... | collective-permute-start | bytes 589832 | tf_op jit(solution)/shard_map/ppermute | solution.py:32
  31.8 0.7 copy-start
  35.3 0.7 copy-start.1

commit v2 on v1

--- a/solution.py
+++ b/solution.py
@@ -30,6 +30,18 @@
 
 def swapped(value, axis):
     return lax.ppermute(value, axis, [(s, s ^ 1) for s in range(lax.axis_size(axis))])
+
+
+def pack_kernel(keep, ids, out):
+    ndev, nframe, lanes = out.shape
+    row = lax.broadcasted_iota(jnp.int32, (nframe, lanes), 0)
+    lane = lax.broadcasted_iota(jnp.int32, (nframe, lanes), 1)
+    block = jnp.zeros((nframe, lanes), F32)
+    for f in range(nframe):
+        value = jnp.where(lane < lanes // 2, keep[f], ids[f].astype(F32))
+        block = jnp.where(row == f, value, block)
+    for d in range(ndev):
+        out[d] = block
 
 
 def table_kernel(packed, rate, scaled, high, low, counts, E):
@@ -76,7 +88,7 @@
     return upper, (value - upper.astype(F32)).astype(BF16)
 
 
-def spread(high, low, scaled, last, pooled, sends, own):
+def spread_kernel(high, low, scaled, last, pooled, sends, own):
     nlat, nproj, nchan = high.shape
     ndev = sends.shape[0]
     width = last.shape[0]
@@ -104,8 +116,8 @@
 
 
 def conv_kernel(
-    window, keep, x_hbm, halo_hbm, own_w, da, db, dc, sa, sb, sc, decay, high, low, scaled,
-    feat_hbm, sends, own, w, X, HA, HB, FA, FB, R, last, pooled, wsem, insem, outsem, *, shards,
+    ids, keep, x_hbm, halo_hbm, own_w, da, db, dc, sa, sb, sc, decay,
+    feat_hbm, last, pooled, w, X, HA, HB, FA, FB, R, wsem, insem, outsem, *, shards,
 ):
     nframe, npos, nchan = x_hbm.shape
     tiles, groups = npos // TILE, nframe // GROUP
@@ -115,6 +127,7 @@
     me = lax.axis_index("dp")
     side = lax.rem(lax.axis_index("tm"), 2)
     lead = KT - 1
+    base = lax.axis_index("tm") * (nframe // STRIDE)
 
     def weights():
         copies = [pltpu.make_async_copy(own_w, w.at[:, pl.ds(pl.multiple_of(me * depth, depth), depth)], wsem.at[0])]
@@ -171,7 +184,7 @@
             v = F[s][g, r : r + SUB, :].astype(F32)
             v = jnp.concatenate([v[:, n : n + 128] * scale for n in range(0, nchan, 128)], 1)
             state = state * (decay[...] * keep[f + g]) + v
-            pooled[window[f + g], rows, :] += state
+            pooled[ids[f + g] - base, rows, :] += state
         last[rows, :] = state
 
     products = [(m, n) for m in range(GROUP * TILE // ROWS) for n in range(0, nchan, 256)]
@@ -224,7 +237,6 @@
         return 0
 
     lax.fori_loop(0, total // 2, body, 0)
-    spread(high, low, scaled, last, pooled, sends, own)
     leaving(total - 2, 0).wait()
     leaving(total - 1, 1).wait()
 
@@ -262,15 +274,20 @@
     own_w = w_time * jnp.asarray(0.5, BF16)
     half = own_w.shape[1] // 2
     mine = lax.dynamic_slice_in_dim(own_w, side * half, half, 1)
-    dc, da, db = rotated(mine, "dp", 2), rotated(mine, "dp", 1), rotated(mine, "dp", -1)
+    dc = rotated(mine, "dp", 2)
+    da = rotated(mine, "dp", 1)
+    db = rotated(mine, "dp", -1)
     sa, sb, sc = swapped(da, "tm"), swapped(db, "tm"), swapped(dc, "tm")
-    source, keep, latent_ids, rate, gain, w_lat, _ = lax.optimization_barrier(
-        (x, keep, latent_ids, rate, gain, w_lat, mine)
-    )
+    source, rate, gain, w_lat, _ = lax.optimization_barrier((x, rate, gain, w_lat, mine))
     halo = shifted(source[nframe - (KT - 1) :], "tm", 1)
-    lane = jnp.arange(128, dtype=jnp.int32)[None]
-    local = jnp.where(lane < 64, keep[:, None], latent_ids.astype(F32)[:, None])
-    local = jnp.broadcast_to(local[None], (ndev, nframe, 128))
+    local = pl.pallas_call(
+        pack_kernel,
+        out_shape=jax.ShapeDtypeStruct((ndev, nframe, 128), F32),
+        in_specs=[pl.BlockSpec(memory_space=pltpu.SMEM)] * 2,
+        out_specs=pl.BlockSpec(memory_space=pltpu.VMEM),
+        compiler_params=pltpu.CompilerParams(vmem_limit_bytes=8 << 20),
+        name="pack",
+    )(keep, latent_ids)
     packed = lax.all_to_all(local, "tm", 0, 0).reshape(nall, 128)
 
     decay = jnp.exp(-rate)[None]
@@ -282,28 +299,15 @@
     hbm = pl.BlockSpec(memory_space=pltpu.HBM)
     table_shape = jax.ShapeDtypeStruct((nlat, nproj, nchan), BF16)
 
-    window = latent_ids - me.astype(jnp.int32) * per
-    high, low, counts = pl.pallas_call(
-        table_kernel,
-        out_shape=(table_shape, table_shape, jax.ShapeDtypeStruct((per, 128), F32)),
-        in_specs=[vmem] * 3,
-        out_specs=(vmem,) * 3,
-        scratch_shapes=[pltpu.VMEM((nall, nchan), F32)],
-        compiler_params=pltpu.CompilerParams(vmem_limit_bytes=24 << 20),
-        cost_estimate=pl.CostEstimate(
-            flops=12 * nlat * nall * nchan, bytes_accessed=4 << 20, transcendentals=nall * nchan
-        ),
-        name="tables",
-    )(packed, rate[None], scaled)
     stage_rows = GROUP * TILE
-    features, sends, own = pl.pallas_call(
+    conv = pl.pallas_call(
         functools.partial(conv_kernel, shards=shards),
         out_shape=(
             jax.ShapeDtypeStruct((nframe, npos, nchan), BF16),
-            jax.ShapeDtypeStruct((ndev, per * nproj, npos), BF16),
-            jax.ShapeDtypeStruct((per * nproj, npos), F32),
+            jax.ShapeDtypeStruct((npos, nchan), F32),
+            jax.ShapeDtypeStruct((3, npos, nchan), F32),
         ),
-        in_specs=[smem, smem] + [hbm] * 9 + [vmem] * 4,
+        in_specs=[smem, smem] + [hbm] * 9 + [vmem],
         out_specs=(hbm, vmem, vmem),
         scratch_shapes=[
             pltpu.VMEM((KT, nchan, nchan), BF16),
@@ -313,20 +317,43 @@
             pltpu.VMEM((GROUP, TILE, nchan), BF16),
             pltpu.VMEM((GROUP, TILE, nchan), BF16),
             pltpu.VMEM((stage_rows, 128), F32),
-            pltpu.VMEM((npos, nchan), F32),
-            pltpu.VMEM((3, npos, nchan), F32),
             pltpu.SemaphoreType.DMA((7,)),
             pltpu.SemaphoreType.DMA((2 * npos // TILE,)),
             pltpu.SemaphoreType.DMA((2,)),
         ],
-        compiler_params=pltpu.CompilerParams(vmem_limit_bytes=44 << 20),
+        compiler_params=pltpu.CompilerParams(vmem_limit_bytes=48 << 20),
         cost_estimate=pl.CostEstimate(
             flops=2 * KT * nframe * npos * nchan * nchan,
             bytes_accessed=4 * nframe * npos * nchan,
             transcendentals=nframe * npos * nchan,
         ),
         name="conv",
-    )(window, keep, x, halo, own_w, da, db, dc, sa, sb, sc, decay, high, low, scaled)
+    )
+    features, last, pooled = conv(latent_ids, keep, x, halo, own_w, da, db, dc, sa, sb, sc, decay)
+    packed, last = lax.optimization_barrier((packed, last))
+    high, low, counts = pl.pallas_call(
+        table_kernel,
+        out_shape=(table_shape, table_shape, jax.ShapeDtypeStruct((per, 128), F32)),
+        in_specs=[vmem] * 3,
+        out_specs=(vmem,) * 3,
+        scratch_shapes=[pltpu.VMEM((nall, nchan), F32)],
+        compiler_params=pltpu.CompilerParams(vmem_limit_bytes=16 << 20),
+        cost_estimate=pl.CostEstimate(
+            flops=12 * nlat * nall * nchan, bytes_accessed=4 << 20, transcendentals=nall * nchan
+        ),
+        name="tables",
+    )(packed, rate[None], scaled)
+    sends, own = pl.pallas_call(
+        spread_kernel,
+        out_shape=(
+            jax.ShapeDtypeStruct((ndev, per * nproj, npos), BF16),
+            jax.ShapeDtypeStruct((per * nproj, npos), F32),
+        ),
+        in_specs=[vmem] * 5,
+        out_specs=(vmem, vmem),
+        compiler_params=pltpu.CompilerParams(vmem_limit_bytes=24 << 20),
+        name="spread",
+    )(high, low, scaled, last, pooled)
     outs = [lax.all_to_all(sends, "tm", 0, 0), own]
     latents = pl.pallas_call(
         final_kernel,

time: 88 us -> 89.7 us (1.019)
  waiting for transfers between devices: 6.61 us -> 0.54 us
  blocking collectives: 20.6 us -> 24.2 us
  Pallas kernels: 33.7 us -> 37.2 us
  local copies, waits for them, and re-layouts: 4.34 us -> 6.5 us
  other arithmetic: 3.93 us -> 2.47 us
    all_to_all x1, waiting for transfers between devices: 6.59 us -> 0.01 us  [per_device(): packed = lax.all_to_all(local, 'tm', 0, 0).reshape(nall, 128)]
    all_to_all x1, blocking collectives: 20.6 us -> 24.2 us  [per_device(): outs = [lax.all_to_all(sends, 'tm', 0, 0), own]]
    pallas_call x1 -> x3, Pallas kernels: 30.1 us -> 33.6 us  [the longest x1 29.4 us: per_device(): conv(latent_ids, keep, x, halo, own_w, da, db, dc, sa, sb, sc, decay)]
    unnamed x4 -> x12, local copies, waits for them, and re-layouts: 1.33 us -> 4.51 us
    slice x1, local copies, waits for them, and re-layouts: 2.27 us -> 1.29 us  [per_device(): halo = shifted(source[nframe - (KT - 1):], 'tm', 1)]
  transfers between devices with their start and end apart: 8 -> 8, of which waited for: 1 -> 2; matrix products, arithmetic and copies ran while one was open for 4% -> 2% of each run, Pallas kernels for 3% -> 34%
where the time goes in v2:
time: 89.7 us; the launch traced here: 89.2 us
  Pallas kernels  37.2 us (41%)
  blocking collectives  24.2 us (27%)
  starting transfers between devices  17.6 us (20%)
  local copies, waits for them, and re-layouts  6.5 us (7%)
  other arithmetic  2.47 us (3%)
    pallas_call x1, Pallas kernels, per_device(): conv(latent_ids, keep, x, halo, own_w, da, db, dc, sa, sb, sc, decay)  29.4 us
    all_to_all x1, blocking collectives, per_device(): outs = [lax.all_to_all(sends, 'tm', 0, 0), own]  24.2 us
    all_to_all x1, starting transfers between devices, per_device(): packed = lax.all_to_all(local, 'tm', 0, 0).reshape(nall, 128)  7.92 us
    ppermute x1, starting transfers between devices, shifted(): lax.ppermute(value, axis, [(s, s + steps) for s in range(count - steps)])  4.58 us
    unnamed x12, local copies, waits for them, and re-layouts  4.51 us
    ppermute x3, starting transfers between devices, rotated(): lax.ppermute(value, axis, [(s, (s + steps) % count) for s in range(count)])  4.28 us
    pallas_call x1, Pallas kernels, per_device(): pl.pallas_call(spread_kernel, out_shape=(jax.ShapeDtypeStruct((ndev, per...  2.98 us
    pallas_call x1, Pallas kernels, per_device(): pl.pallas_call(table_kernel, out_shape=(table_shape, table_shape, jax.Sha...  2.77 us
  transfers between devices with their start and end apart: 8, of which 2 were waited for; matrix products, arithmetic and copies ran while one was open for 2% of the time, Pallas kernels for 34%

profile of v2, /device:TPU:1, one launch (start us, length us, event | category | flops | bytes accessed | tf_op | source)
XLA Modules:
  0.0 89.2 jit_solution(6093589799761360600)
XLA Ops:
  0.6 1.0 %broadcast_multiply_fusion.own_w = bf16[3,128,512]{2,1,0:T(8,128)(2,1)S(1)} fusion(bf16[3,128,512]{2,1,0:T(8,128)(2,1)} %param.8), kind=kLoop, calls=%fused_computation | loop fusion | flops 196608 | bytes 786432 | tf_op jit(solution)/shard_map/mul | solution.py:274
  1.7 0.7 constant_dynamic-slice_fusion
  2.4 1.3 %slice.3 = bf16[2,512,512]{2,1,0:T(8,128)(2,1)S(1)} slice(bf16[16,512,512]{2,1,0:T(8,128)(2,1)} %bitcast.11), slice={[14:16], [0:512], [0:512]} | slice | bytes 2097152 | tf_op jit(solution)/shard_map/slice | solution.py:282
  3.7 4.6 %collective-permute-start = (bf16[2,512,512]{2,1,0:T(8,128)(2,1)S(1)}, bf16[2,512,512]{2,1,0:T(8,128)(2,1)S(1)}, u32[]{:S(2)}, u32[]{:S(2)}) collective-permute-start(bf16[2,512,512]{2,1,0:T(8,128)(2,1)S(1)} %slice.3), channel_id=1, source_target_pairs={{0,1},{1,2},{2,3},{3,4},{4,5},{5,6},{6,7},{7,8},{8,9},{9,10},{10,1... | collective-permute-start | bytes 3145736 | tf_op jit(solution)/shard_map/ppermute | solution.py:28
  8.3 1.3 %collective-permute-start.1 = (bf16[3,64,512]{2,1,0:T(8,128)(2,1)}, bf16[3,64,512]{2,1,0:T(8,128)(2,1)S(1)}, u32[]{:S(2)}, u32[]{:S(2)}) collective-permute-start(bf16[3,64,512]{2,1,0:T(8,128)(2,1)} %constant_dynamic-slice_fusion), channel_id=1, source_target_pairs={{0,32},{32,64},{64,96},{96,0},{1,33},{33,65},{65,97},{97,1},{2,34}... | collective-permute-start | bytes 589832 | tf_op jit(solution)/shard_map/ppermute | solution.py:23
  9.6 1.5 %collective-permute-start.2 = (bf16[3,64,512]{2,1,0:T(8,128)(2,1)}, bf16[3,64,512]{2,1,0:T(8,128)(2,1)S(1)}, u32[]{:S(2)}, u32[]{:S(2)}) collective-permute-start(bf16[3,64,512]{2,1,0:T(8,128)(2,1)} %constant_dynamic-slice_fusion), channel_id=1, source_target_pairs={{0,96},{32,0},{64,32},{96,64},{1,97},{33,1},{65,33},{97,65},{2,98}... | collective-permute-start | bytes 589832 | tf_op jit(solution)/shard_map/ppermute | solution.py:23
  11.0 1.5 %collective-permute-start.3 = (bf16[3,64,512]{2,1,0:T(8,128)(2,1)}, bf16[3,64,512]{2,1,0:T(8,128)(2,1)S(1)}, u32[]{:S(2)}, u32[]{:S(2)}) collective-permute-start(bf16[3,64,512]{2,1,0:T(8,128)(2,1)} %constant_dynamic-slice_fusion), channel_id=1, source_target_pairs={{0,64},{32,96},{64,0},{96,32},{1,65},{33,97},{65,1},{97,33},{2,66}... | collective-permute-start | bytes 589832 | tf_op jit(solution)/shard_map/ppermute | solution.py:23
  12.6 0.0 copy-start.2
  12.6 0.7 copy-done.2
  13.2 0.0 copy-start.4
  13.2 0.7 copy-done.4
  13.9 1.3 %pack.1 = f32[32,16,128]{2,1,0:T(8,128)} custom-call(f32[16]{0:T(128)S(1)} %copy-done.4, s32[16]{0:T(128)S(1)} %copy-done.2), custom_call_target="tpu_custom_call" | custom-call | tf_op jit(solution)/shard_map/pack/pallas_call | solution.py:283
  15.2 7.9 %all-to-all-start = ((f32[32,16,128]{2,1,0:T(8,128)}), f32[32,16,128]{2,1,0:T(8,128)S(1)}, u32[]{:S(2)}, u32[]{:S(2)}) async-start(f32[32,16,128]{2,1,0:T(8,128)} %pack.1), calls=%async_computation | async-start | bytes 524288 | tf_op jit(solution)/shard_map/all_to_all | solution.py:291
  23.1 0.7 sqrt_multiply_fusion
  23.8 0.0 collective-permute-done.1.da
  23.8 0.3 collective-permute-start.4
  24.1 0.0 collective-permute-done.2.db
  24.1 0.3 collective-permute-start.5
  24.4 0.0 collective-permute-done.3.dc
  24.4 0.2 collective-permute-start.6
  24.6 0.7 multiply_bitcast_fusion.scaled
  25.4 0.0 collective-permute-done.4.sa
  25.4 0.2 collective-permute-done.5.sb
  25.6 0.3 collective-permute-done.6.sc
  25.9 0.0 collective-permute-done.halo_hbm
  25.9 0.0 copy-start.3
  25.9 0.7 copy-done.3
  26.5 0.0 copy-start.5
  26.5 0.7 copy-done.5
  27.2 0.0 copy-start.1
  27.2 29.4 %conv.1 = (bf16[16,512,512]{2,1,0:T(8,128)(2,1)}, f32[512,512]{1,0:T(8,128)S(1)}, f32[3,512,512]{2,1,0:T(8,128)}) custom-call(s32[16]{0:T(128)S(1)} %copy-done.3, f32[16]{0:T(128)S(1)} %copy-done.5, bf16[16,512,512]{2,1,0:T(8,128)(2,1)} %bitcast.12, bf16[2,512,512]{2,1,0:T(8,128)(2,1)S(1)} %collective-permute-done.halo_hbm, ...), custom_call_target="tpu_custom_call" | custom-call | flops 12884901888 | bytes 16777216 | tf_op jit(solution)/shard_map/conv/pallas_call | solution.py:332
  56.6 0.0 all-to-all-done
  56.6 0.0 copy-done.1
  56.6 2.8 %tables.1 = (bf16[64,16,512]{2,1,0:T(8,128)(2,1)S(1)}, bf16[64,16,512]{2,1,0:T(8,128)(2,1)S(1)}, f32[2,128]{1,0:T(2,128)S(1)}) custom-call(f32[512,128]{1,0:T(8,128)S(1)} %bitcast.8, f32[1,512]{1,0:T(1,128)S(1)} %bitcast.9, f32[16,512]{1,0:T(8,128)S(1)} %multiply_bitcast_fusion.scaled), custom_call_target="tpu_custom_call" | custom-call | flops 201326592 | bytes 4194304 | tf_op jit(solution)/shard_map/tables/pallas_call | solution.py:334
  59.4 0.0 copy-start
  59.4 1.9 %copy-done = f32[3,512,512]{2,1,0:T(8,128)S(1)} copy-done((f32[3,512,512]{2,1,0:T(8,128)S(1)}, f32[3,512,512]{2,1,0:T(8,128)}, u32[]{:S(2)}) %copy-start) | copy-done | bytes 3145752
  61.3 3.0 %spread.1 = (bf16[32,32,512]{2,1,0:T(8,128)(2,1)S(1)}, f32[32,512]{1,0:T(8,128)S(1)}) custom-call(bf16[64,16,512]{2,1,0:T(8,128)(2,1)S(1)} %get-tuple-element.24.high, bf16[64,16,512]{2,1,0:T(8,128)(2,1)S(1)} %get-tuple-element.25.low, f32[16,512]{1,0:T(8,128)S(1)} %multiply_bitcast_fusion.scaled, f32[512,512]{1,0:T(8,128)S(1)} %get-tuple-element.26.last, ...), custom_call_target="tpu_custom_call" | custom-call | tf_op jit(solution)/shard_map/spread/pallas_call | solution.py:346
  64.2 24.2 %all_to_all.10.refs_0_ = bf16[32,32,512]{2,1,0:T(8,128)(2,1)S(1)} all-to-all(bf16[32,32,512]{2,1,0:T(8,128)(2,1)S(1)} %get-tuple-element.28), channel_id=1, replica_groups=mesh['dp'=4,'tm'=32] {'tm'}, dimensions={0} | all-to-all | bytes 2097152 | tf_op jit(solution)/shard_map/all_to_all | solution.py:357
  88.4 0.8 final.1
Async XLA Ops:
  3.7 22.2 %collective-permute-start = (bf16[2,512,512]{2,1,0:T(8,128)(2,1)S(1)}, bf16[2,512,512]{2,1,0:T(8,128)(2,1)S(1)}, u32[]{:S(2)}, u32[]{:S(2)}) collective-permute-start(bf16[2,512,512]{2,1,0:T(8,128)(2,1)S(1)} %slice.3), channel_id=1, source_target_pairs={{0,1},{1,2},{2,3},{3,4},{4,5},{5,6},{6,7},{7,8},{8,9},{9,10},{10,1... | collective-permute-start | bytes 3145736 | tf_op jit(solution)/shard_map/ppermute | solution.py:28
  8.3 15.5 %collective-permute-start.1 = (bf16[3,64,512]{2,1,0:T(8,128)(2,1)}, bf16[3,64,512]{2,1,0:T(8,128)(2,1)S(1)}, u32[]{:S(2)}, u32[]{:S(2)}) collective-permute-start(bf16[3,64,512]{2,1,0:T(8,128)(2,1)} %constant_dynamic-slice_fusion), channel_id=1, source_target_pairs={{0,32},{32,64},{64,96},{96,0},{1,33},{33,65},{65,97},{97,1},{2,34}... | collective-permute-start | bytes 589832 | tf_op jit(solution)/shard_map/ppermute | solution.py:23
  9.6 14.6 %collective-permute-start.2 = (bf16[3,64,512]{2,1,0:T(8,128)(2,1)}, bf16[3,64,512]{2,1,0:T(8,128)(2,1)S(1)}, u32[]{:S(2)}, u32[]{:S(2)}) collective-permute-start(bf16[3,64,512]{2,1,0:T(8,128)(2,1)} %constant_dynamic-slice_fusion), channel_id=1, source_target_pairs={{0,96},{32,0},{64,32},{96,64},{1,97},{33,1},{65,33},{97,65},{2,98}... | collective-permute-start | bytes 589832 | tf_op jit(solution)/shard_map/ppermute | solution.py:23
  11.0 13.4 %collective-permute-start.3 = (bf16[3,64,512]{2,1,0:T(8,128)(2,1)}, bf16[3,64,512]{2,1,0:T(8,128)(2,1)S(1)}, u32[]{:S(2)}, u32[]{:S(2)}) collective-permute-start(bf16[3,64,512]{2,1,0:T(8,128)(2,1)} %constant_dynamic-slice_fusion), channel_id=1, source_target_pairs={{0,64},{32,96},{64,0},{96,32},{1,65},{33,97},{65,1},{97,33},{2,66}... | collective-permute-start | bytes 589832 | tf_op jit(solution)/shard_map/ppermute | solution.py:23
  12.6 0.7 copy-start.2
  13.2 0.7 copy-start.4
  15.2 41.4 %all-to-all-start = ((f32[32,16,128]{2,1,0:T(8,128)}), f32[32,16,128]{2,1,0:T(8,128)S(1)}, u32[]{:S(2)}, u32[]{:S(2)}) async-start(f32[32,16,128]{2,1,0:T(8,128)} %pack.1), calls=%async_computation | async-start | bytes 524288 | tf_op jit(solution)/shard_map/all_to_all | solution.py:291
  23.8 1.6 %collective-permute-start.4 = (bf16[3,64,512]{2,1,0:T(8,128)(2,1)S(1)}, bf16[3,64,512]{2,1,0:T(8,128)(2,1)S(1)}, u32[]{:S(2)}, u32[]{:S(2)}) collective-permute-start(bf16[3,64,512]{2,1,0:T(8,128)(2,1)S(1)} %collective-permute-done.1.da), channel_id=1, source_target_pairs={{0,1},{1,0},{2,3},{3,2},{4,5},{5,4},{6,7},{7,6},{8,9},{9,8},{10,11... | collective-permute-start | bytes 589832 | tf_op jit(solution)/shard_map/ppermute | solution.py:32
  24.1 1.5 %collective-permute-start.5 = (bf16[3,64,512]{2,1,0:T(8,128)(2,1)S(1)}, bf16[3,64,512]{2,1,0:T(8,128)(2,1)S(1)}, u32[]{:S(2)}, u32[]{:S(2)}) collective-permute-start(bf16[3,64,512]{2,1,0:T(8,128)(2,1)S(1)} %collective-permute-done.2.db), channel_id=1, source_target_pairs={{0,1},{1,0},{2,3},{3,2},{4,5},{5,4},{6,7},{7,6},{8,9},{9,8},{10,11... | collective-permute-start | bytes 589832 | tf_op jit(solution)/shard_map/ppermute | solution.py:32
  24.4 1.5 %collective-permute-start.6 = (bf16[3,64,512]{2,1,0:T(8,128)(2,1)S(1)}, bf16[3,64,512]{2,1,0:T(8,128)(2,1)S(1)}, u32[]{:S(2)}, u32[]{:S(2)}) collective-permute-start(bf16[3,64,512]{2,1,0:T(8,128)(2,1)S(1)} %collective-permute-done.3.dc), channel_id=1, source_target_pairs={{0,1},{1,0},{2,3},{3,2},{4,5},{5,4},{6,7},{7,6},{8,9},{9,8},{10,11... | collective-permute-start | bytes 589832 | tf_op jit(solution)/shard_map/ppermute | solution.py:32
  25.9 0.7 copy-start.3
  26.5 0.7 copy-start.5
  27.2 29.4 %copy-start.1 = (f32[512]{0:T(512)S(1)}, f32[512]{0:T(512)}, u32[]{:S(2)}) copy-start(f32[512]{0:T(512)} %param.10) | copy-start | bytes 6148
  59.4 1.9 %copy-start = (f32[3,512,512]{2,1,0:T(8,128)S(1)}, f32[3,512,512]{2,1,0:T(8,128)}, u32[]{:S(2)}) copy-start(f32[3,512,512]{2,1,0:T(8,128)} %get-tuple-element.27.pooled) | copy-start | bytes 9437188

commit v3 on v2

--- a/solution.py
+++ b/solution.py
@@ -32,16 +32,10 @@
     return lax.ppermute(value, axis, [(s, s ^ 1) for s in range(lax.axis_size(axis))])
 
 
-def pack_kernel(keep, ids, out):
-    ndev, nframe, lanes = out.shape
-    row = lax.broadcasted_iota(jnp.int32, (nframe, lanes), 0)
-    lane = lax.broadcasted_iota(jnp.int32, (nframe, lanes), 1)
-    block = jnp.zeros((nframe, lanes), F32)
-    for f in range(nframe):
-        value = jnp.where(lane < lanes // 2, keep[f], ids[f].astype(F32))
-        block = jnp.where(row == f, value, block)
-    for d in range(ndev):
-        out[d] = block
+def pieces_of(value):
+    one = value.astype(BF16).astype(F32)
+    two = (value - one).astype(BF16).astype(F32)
+    return one, two, value - one - two
 
 
 def table_kernel(packed, rate, scaled, high, low, counts, E):
@@ -51,22 +45,27 @@
     me = lax.axis_index("tm")
     end = (me + 1) * (nall // lax.axis_size("tm")) - 1
     frame = lax.broadcasted_iota(jnp.int32, (nall, lanes), 0)
-    logs = jnp.where(frame > end, jnp.log(jnp.maximum(packed[...], 0.5)), 0.0)
+    lane = lax.broadcasted_iota(jnp.int32, (nall, lanes), 1)
+    logs = jnp.where(frame > end, jnp.log(packed[:, 0:1]), 0.0)
+    one, two, three = pieces_of(logs)
+    pieces = jnp.where(lane == 0, one, jnp.where(lane == 1, two, jnp.where(lane == 2, three, 0.0)))
     rows = lax.broadcasted_iota(jnp.int32, (nall, nall), 0)
     cols = lax.broadcasted_iota(jnp.int32, (nall, nall), 1)
-    run = jnp.dot(
-        (cols <= rows).astype(F32), logs, precision=lax.Precision.HIGHEST, preferred_element_type=F32
-    )
+    lower = jnp.where(cols <= rows, 1.0, 0.0).astype(BF16)
+    run = jnp.dot(lower, pieces.astype(BF16), preferred_element_type=F32)
+    run = jnp.sum(run, -1, keepdims=True)
     block = 128
     for r in range(0, nall, block):
         at = lax.broadcasted_iota(jnp.int32, (block, nchan), 0) + r
         gap = (at - end).astype(F32)
-        E[r : r + block, :] = jnp.where(at > end, jnp.exp(run[r : r + block, 0:1] - rate[...] * gap), 0.0)
+        E[r : r + block, :] = jnp.where(at > end, jnp.exp(run[r : r + block] - rate[...] * gap), 0.0)
     ids = packed[:, lanes // 2 : lanes // 2 + 1].astype(jnp.int32)
-    member = (lax.broadcasted_iota(jnp.int32, (nall, lanes), 1) == ids).astype(F32)
-    table = lax.dot_general(
-        member, E[...], (((0,), (0,)), ((), ())), precision=lax.Precision.HIGHEST, preferred_element_type=F32
-    )
+    member = jnp.where(lane == ids, 1.0, 0.0).astype(BF16)
+    table = jnp.zeros((lanes, nchan), F32)
+    for piece in pieces_of(E[...]):
+        table = table + lax.dot_general(
+            member, piece.astype(BF16), (((0,), (0,)), ((), ())), preferred_element_type=F32
+        )
     per = counts.shape[0]
     for i in range(per):
         hit = (jnp.broadcast_to(ids, (nall, lanes)) == me * per + i).astype(F32)
@@ -88,36 +87,28 @@
     return upper, (value - upper.astype(F32)).astype(BF16)
 
 
-def spread_kernel(high, low, scaled, last, pooled, sends, own):
+def spread_kernel(high, low, last, own, sends):
     nlat, nproj, nchan = high.shape
-    ndev = sends.shape[0]
-    width = last.shape[0]
+    ndev, per, width = sends.shape
     top, rest = split(last[...])
     rows = 256
-    per = sends.shape[1]
     for r in range(0, nlat * nproj, rows):
         upper = high[r // nproj : (r + rows) // nproj].reshape(rows, nchan)
         lower = low[r // nproj : (r + rows) // nproj].reshape(rows, nchan)
         z = times(upper, top) + times(upper, rest) + times(lower, top)
         sends[r // per : (r + rows) // per] = z.reshape(rows // per, per, width).astype(BF16)
-    upper, lower = split(scaled[...])
-    parts = []
-    for j in range(3):
-        top, rest = split(pooled[j])
-        parts.append(times(upper, top) + times(upper, rest) + times(lower, top))
-    own[0:nproj, :] = parts[0]
-    own[nproj : 2 * nproj, :] = parts[1]
     me = lax.axis_index("tm")
 
     @pl.when(me < ndev - 1)
     def _():
         block = sends[me + 1]
-        sends[me + 1, 0:nproj] = (block[0:nproj].astype(F32) + parts[2]).astype(BF16)
+        moved = own[2 * nproj : 3 * nproj, :]
+        sends[me + 1, 0:nproj] = (block[0:nproj].astype(F32) + moved).astype(BF16)
 
 
 def conv_kernel(
-    ids, keep, x_hbm, halo_hbm, own_w, da, db, dc, sa, sb, sc, decay,
-    feat_hbm, last, pooled, w, X, HA, HB, FA, FB, R, wsem, insem, outsem, *, shards,
+    window, keep, x_hbm, halo_hbm, own_w, da, db, dc, sa, sb, sc, decay, scaled,
+    feat_hbm, last, sums, w, X, HA, HB, FA, FB, R, pooled, wsem, insem, outsem, *, shards,
 ):
     nframe, npos, nchan = x_hbm.shape
     tiles, groups = npos // TILE, nframe // GROUP
@@ -127,7 +118,6 @@
     me = lax.axis_index("dp")
     side = lax.rem(lax.axis_index("tm"), 2)
     lead = KT - 1
-    base = lax.axis_index("tm") * (nframe // STRIDE)
 
     def weights():
         copies = [pltpu.make_async_copy(own_w, w.at[:, pl.ds(pl.multiple_of(me * depth, depth), depth)], wsem.at[0])]
@@ -184,7 +174,7 @@
             v = F[s][g, r : r + SUB, :].astype(F32)
             v = jnp.concatenate([v[:, n : n + 128] * scale for n in range(0, nchan, 128)], 1)
             state = state * (decay[...] * keep[f + g]) + v
-            pooled[ids[f + g] - base, rows, :] += state
+            pooled[window[f + g], rows, :] += state
         last[rows, :] = state
 
     products = [(m, n) for m in range(GROUP * TILE // ROWS) for n in range(0, nchan, 256)]
@@ -237,6 +227,13 @@
         return 0
 
     lax.fori_loop(0, total // 2, body, 0)
+    nproj = scaled.shape[0]
+    upper, lower = split(scaled[...])
+    both = jnp.concatenate([upper, lower], 0)
+    for j in range(3):
+        top, rest = split(pooled[j])
+        part = times(both, top)
+        sums[j * nproj : (j + 1) * nproj, :] = part[:nproj] + part[nproj:] + times(upper, rest)
     leaving(total - 2, 0).wait()
     leaving(total - 1, 1).wait()
 
@@ -278,16 +275,13 @@
     da = rotated(mine, "dp", 1)
     db = rotated(mine, "dp", -1)
     sa, sb, sc = swapped(da, "tm"), swapped(db, "tm"), swapped(dc, "tm")
-    source, rate, gain, w_lat, _ = lax.optimization_barrier((x, rate, gain, w_lat, mine))
-    halo = shifted(source[nframe - (KT - 1) :], "tm", 1)
-    local = pl.pallas_call(
-        pack_kernel,
-        out_shape=jax.ShapeDtypeStruct((ndev, nframe, 128), F32),
-        in_specs=[pl.BlockSpec(memory_space=pltpu.SMEM)] * 2,
-        out_specs=pl.BlockSpec(memory_space=pltpu.VMEM),
-        compiler_params=pltpu.CompilerParams(vmem_limit_bytes=8 << 20),
-        name="pack",
-    )(keep, latent_ids)
+    rate, gain, w_lat, _ = lax.optimization_barrier((rate, gain, w_lat, mine))
+    halo = shifted(x[nframe - (KT - 1) :], "tm", 1)
+    window = latent_ids - me.astype(jnp.int32) * per
+    keep = jnp.where(latent_ids < 0, 0.0, keep)
+    lane = jnp.arange(128, dtype=jnp.int32)[None]
+    local = jnp.where(lane < 64, keep[:, None], latent_ids.astype(F32)[:, None])
+    local = jnp.broadcast_to(local[None], (ndev, nframe, 128))
     packed = lax.all_to_all(local, "tm", 0, 0).reshape(nall, 128)
 
     decay = jnp.exp(-rate)[None]
@@ -305,9 +299,9 @@
         out_shape=(
             jax.ShapeDtypeStruct((nframe, npos, nchan), BF16),
             jax.ShapeDtypeStruct((npos, nchan), F32),
-            jax.ShapeDtypeStruct((3, npos, nchan), F32),
+            jax.ShapeDtypeStruct((3 * nproj, npos), F32),
         ),
-        in_specs=[smem, smem] + [hbm] * 9 + [vmem],
+        in_specs=[smem, smem] + [hbm] * 9 + [vmem] * 2,
         out_specs=(hbm, vmem, vmem),
         scratch_shapes=[
             pltpu.VMEM((KT, nchan, nchan), BF16),
@@ -317,6 +311,7 @@
             pltpu.VMEM((GROUP, TILE, nchan), BF16),
             pltpu.VMEM((GROUP, TILE, nchan), BF16),
             pltpu.VMEM((stage_rows, 128), F32),
+            pltpu.VMEM((3, npos, nchan), F32),
             pltpu.SemaphoreType.DMA((7,)),
             pltpu.SemaphoreType.DMA((2 * npos // TILE,)),
             pltpu.SemaphoreType.DMA((2,)),
@@ -329,7 +324,7 @@
         ),
         name="conv",
     )
-    features, last, pooled = conv(latent_ids, keep, x, halo, own_w, da, db, dc, sa, sb, sc, decay)
+    features, last, own = conv(window, keep, x, halo, own_w, da, db, dc, sa, sb, sc, decay, scaled)
     packed, last = lax.optimization_barrier((packed, last))
     high, low, counts = pl.pallas_call(
         table_kernel,
@@ -343,17 +338,14 @@
         ),
         name="tables",
     )(packed, rate[None], scaled)
-    sends, own = pl.pallas_call(
+    sends = pl.pallas_call(
         spread_kernel,
-        out_shape=(
-            jax.ShapeDtypeStruct((ndev, per * nproj, npos), BF16),
-            jax.ShapeDtypeStruct((per * nproj, npos), F32),
-        ),
-        in_specs=[vmem] * 5,
-        out_specs=(vmem, vmem),
-        compiler_params=pltpu.CompilerParams(vmem_limit_bytes=24 << 20),
+        out_shape=jax.ShapeDtypeStruct((ndev, per * nproj, npos), BF16),
+        in_specs=[vmem] * 4,
+        out_specs=vmem,
+        compiler_params=pltpu.CompilerParams(vmem_limit_bytes=16 << 20),
         name="spread",
-    )(high, low, scaled, last, pooled)
+    )(high, low, last, own)
     outs = [lax.all_to_all(sends, "tm", 0, 0), own]
     latents = pl.pallas_call(
         final_kernel,

time: 89.7 us -> 85.5 us (0.953)
  Pallas kernels: 37.2 us -> 32.1 us
  local copies, waits for them, and re-layouts: 6.5 us -> 2.71 us
  blocking collectives: 24.2 us -> 26.7 us
  other arithmetic: 2.47 us -> 3.96 us
    unnamed x12 -> x2, local copies, waits for them, and re-layouts: 4.51 us -> 0.01 us
    pallas_call x3 -> x2, Pallas kernels: 33.6 us -> 29.7 us  [the longest x1 27.9 us: per_device(): conv(window, keep, x, halo, own_w, da, db, dc, sa, sb, sc, decay, scaled)]
    all_to_all x1, blocking collectives: 24.2 us -> 26.7 us  [per_device(): outs = [lax.all_to_all(sends, 'tm', 0, 0), own]]
    pallas_call x1, Pallas kernels: 2.77 us -> 1.56 us  [per_device(): pl.pallas_call(table_kernel, out_shape=(table_shape, table_shape, jax.Sha...]
  transfers between devices with their start and end apart: 8 -> 8, of which waited for: 2 -> 2; matrix products, arithmetic and copies ran while one was open for 2% -> 6% of each run, Pallas kernels for 34% -> 33%
where the time goes in v3:
time: 85.5 us; the launch traced here: 85.1 us
  Pallas kernels  32.1 us (38%)
  blocking collectives  26.7 us (31%)
  starting transfers between devices  18.4 us (22%)
  other arithmetic  3.96 us (5%)
  local copies, waits for them, and re-layouts  2.71 us (3%)
    pallas_call x1, Pallas kernels, per_device(): conv(window, keep, x, halo, own_w, da, db, dc, sa, sb, sc, decay, scaled)  27.9 us
    all_to_all x1, blocking collectives, per_device(): outs = [lax.all_to_all(sends, 'tm', 0, 0), own]  26.7 us
    all_to_all x1, starting transfers between devices, per_device(): packed = lax.all_to_all(local, 'tm', 0, 0).reshape(nall, 128)  7.92 us
    ppermute x3, starting transfers between devices, rotated(): lax.ppermute(value, axis, [(s, (s + steps) % count) for s in range(count)])  5.03 us
    ppermute x1, starting transfers between devices, shifted(): lax.ppermute(value, axis, [(s, s + steps) for s in range(count - steps)])  4.61 us
    pallas_call x1, Pallas kernels, per_device(): pl.pallas_call(spread_kernel, out_shape=jax.ShapeDtypeStruct((ndev, per *...  1.84 us
  transfers between devices with their start and end apart: 8, of which 2 were waited for; matrix products, arithmetic and copies ran while one was open for 6% of the time, Pallas kernels for 33%

profile of v3, /device:TPU:1, one launch (start us, length us, event | category | flops | bytes accessed | tf_op | source)
XLA Modules:
  0.0 85.1 jit_solution(12129276992695966652)
XLA Ops:
  0.6 1.0 %broadcast_multiply_fusion.own_w = bf16[3,128,512]{2,1,0:T(8,128)(2,1)S(1)} fusion(bf16[3,128,512]{2,1,0:T(8,128)(2,1)} %param.8), kind=kLoop, calls=%fused_computation.1 | loop fusion | flops 196608 | bytes 786432 | tf_op jit(solution)/shard_map/mul | solution.py:271
  1.7 0.7 constant_dynamic-slice_fusion
  2.4 3.6 %collective-permute-start.3 = (bf16[3,64,512]{2,1,0:T(8,128)(2,1)}, bf16[3,64,512]{2,1,0:T(8,128)(2,1)S(1)}, u32[]{:S(2)}, u32[]{:S(2)}) collective-permute-start(bf16[3,64,512]{2,1,0:T(8,128)(2,1)} %constant_dynamic-slice_fusion), channel_id=1, source_target_pairs={{0,64},{32,96},{64,0},{96,32},{1,65},{33,97},{65,1},{97,33},{2,66}... | collective-permute-start | bytes 589832 | tf_op jit(solution)/shard_map/ppermute | solution.py:23
  5.9 0.9 %collective-permute-start.2 = (bf16[3,64,512]{2,1,0:T(8,128)(2,1)}, bf16[3,64,512]{2,1,0:T(8,128)(2,1)S(1)}, u32[]{:S(2)}, u32[]{:S(2)}) collective-permute-start(bf16[3,64,512]{2,1,0:T(8,128)(2,1)} %constant_dynamic-slice_fusion), channel_id=1, source_target_pairs={{0,96},{32,0},{64,32},{96,64},{1,97},{33,1},{65,33},{97,65},{2,98}... | collective-permute-start | bytes 589832 | tf_op jit(solution)/shard_map/ppermute | solution.py:23
  6.8 0.6 collective-permute-start.1
  7.4 1.3 %slice_bitcast_fusion = bf16[2,512,512]{2,1,0:T(8,128)(2,1)S(1)} fusion(bf16[1,16,512,512]{3,2,1,0:T(8,128)(2,1)} %param.7), kind=kLoop, calls=%fused_computation | loop fusion | bytes 2097152 | tf_op jit(solution)/shard_map/slice | solution.py:279
  8.7 4.6 %collective-permute-start = (bf16[2,512,512]{2,1,0:T(8,128)(2,1)S(1)}, bf16[2,512,512]{2,1,0:T(8,128)(2,1)S(1)}, u32[]{:S(2)}, u32[]{:S(2)}) collective-permute-start(bf16[2,512,512]{2,1,0:T(8,128)(2,1)S(1)} %slice_bitcast_fusion), channel_id=1, source_target_pairs={{0,1},{1,2},{2,3},{3,4},{4,5},{5,6},{6,7},{7,8},{8,9},{9,10},{10,1... | collective-permute-start | bytes 3145736 | tf_op jit(solution)/shard_map/ppermute | solution.py:28
  13.3 0.7 compare_select_fusion.keep
  14.0 0.7 fusion
  14.7 0.1 broadcast_select_fusion
  14.8 0.7 broadcast_in_dim.56
  15.5 7.9 %all-to-all-start = ((f32[32,16,128]{2,1,0:T(8,128)}), f32[32,16,128]{2,1,0:T(8,128)S(1)}, u32[]{:S(2)}, u32[]{:S(2)}) async-start(f32[32,16,128]{2,1,0:T(8,128)} %broadcast_in_dim.56), calls=%async_computation | async-start | bytes 524288 | tf_op jit(solution)/shard_map/all_to_all | solution.py:285
  23.5 0.7 sqrt_multiply_fusion
  24.2 0.0 collective-permute-done.3.dc
  24.2 0.3 collective-permute-start.6
  24.5 0.0 collective-permute-done.2.db
  24.5 0.3 collective-permute-start.5
  24.8 0.0 collective-permute-done.1.da
  24.8 0.2 collective-permute-start.4
  25.0 0.7 multiply_bitcast_fusion.scaled
  25.7 0.0 collective-permute-done.6.sc
  25.7 0.2 collective-permute-done.5.sb
  26.0 0.3 collective-permute-done.4.sa
  26.3 0.0 collective-permute-done.halo_hbm
  26.3 0.0 copy-start
  26.3 27.9 %conv.1 = (bf16[16,512,512]{2,1,0:T(8,128)(2,1)}, f32[512,512]{1,0:T(8,128)S(1)}, f32[48,512]{1,0:T(8,128)S(1)}) custom-call(s32[16]{0:T(128)S(1)} %get-tuple-element.27.window, f32[16]{0:T(128)S(1)} %compare_select_fusion.keep, bf16[16,512,512]{2,1,0:T(8,128)(2,1)} %bitcast.13, bf16[2,512,512]{2,1,0:T(8,128)(2,1)S(1)} %collective-permute-done.halo_hbm, ...), custom_call_target="tpu_custom_call" | custom-call | flops 12884901888 | bytes 16777216 | tf_op jit(solution)/shard_map/conv/pallas_call | solution.py:327
  54.2 0.0 all-to-all-done
  54.2 0.0 copy-done
  54.2 1.6 %tables.1 = (bf16[64,16,512]{2,1,0:T(8,128)(2,1)S(1)}, bf16[64,16,512]{2,1,0:T(8,128)(2,1)S(1)}, f32[2,128]{1,0:T(2,128)S(1)}) custom-call(f32[512,128]{1,0:T(8,128)S(1)} %bitcast.10, f32[1,512]{1,0:T(1,128)S(1)} %bitcast.11, f32[16,512]{1,0:T(8,128)S(1)} %multiply_bitcast_fusion.scaled), custom_call_target="tpu_custom_call" | custom-call | flops 201326592 | bytes 4194304 | tf_op jit(solution)/shard_map/tables/pallas_call | solution.py:329
  55.8 1.8 %spread.1 = bf16[32,32,512]{2,1,0:T(8,128)(2,1)S(1)} custom-call(bf16[64,16,512]{2,1,0:T(8,128)(2,1)S(1)} %get-tuple-element.20.high, bf16[64,16,512]{2,1,0:T(8,128)(2,1)S(1)} %get-tuple-element.21.low, f32[512,512]{1,0:T(8,128)S(1)} %get-tuple-element.22.last, f32[48,512]{1,0:T(8,128)S(1)} %get-tuple-element.23.own.refs_1_), custom_call_target="tpu_custom_call" | custom-call | tf_op jit(solution)/shard_map/spread/pallas_call | solution.py:341
  57.6 26.7 %all_to_all.10.refs_0_ = bf16[32,32,512]{2,1,0:T(8,128)(2,1)S(1)} all-to-all(bf16[32,32,512]{2,1,0:T(8,128)(2,1)S(1)} %spread.1), channel_id=1, replica_groups=mesh['dp'=4,'tm'=32] {'tm'}, dimensions={0} | all-to-all | bytes 2097152 | tf_op jit(solution)/shard_map/all_to_all | solution.py:349
  84.3 0.8 final.1
  (1 shorter events, 0.0 us)
Async XLA Ops:
  2.4 21.8 %collective-permute-start.3 = (bf16[3,64,512]{2,1,0:T(8,128)(2,1)}, bf16[3,64,512]{2,1,0:T(8,128)(2,1)S(1)}, u32[]{:S(2)}, u32[]{:S(2)}) collective-permute-start(bf16[3,64,512]{2,1,0:T(8,128)(2,1)} %constant_dynamic-slice_fusion), channel_id=1, source_target_pairs={{0,64},{32,96},{64,0},{96,32},{1,65},{33,97},{65,1},{97,33},{2,66}... | collective-permute-start | bytes 589832 | tf_op jit(solution)/shard_map/ppermute | solution.py:23
  5.9 18.6 %collective-permute-start.2 = (bf16[3,64,512]{2,1,0:T(8,128)(2,1)}, bf16[3,64,512]{2,1,0:T(8,128)(2,1)S(1)}, u32[]{:S(2)}, u32[]{:S(2)}) collective-permute-start(bf16[3,64,512]{2,1,0:T(8,128)(2,1)} %constant_dynamic-slice_fusion), channel_id=1, source_target_pairs={{0,96},{32,0},{64,32},{96,64},{1,97},{33,1},{65,33},{97,65},{2,98}... | collective-permute-start | bytes 589832 | tf_op jit(solution)/shard_map/ppermute | solution.py:23
  6.8 18.0 %collective-permute-start.1 = (bf16[3,64,512]{2,1,0:T(8,128)(2,1)}, bf16[3,64,512]{2,1,0:T(8,128)(2,1)S(1)}, u32[]{:S(2)}, u32[]{:S(2)}) collective-permute-start(bf16[3,64,512]{2,1,0:T(8,128)(2,1)} %constant_dynamic-slice_fusion), channel_id=1, source_target_pairs={{0,32},{32,64},{64,96},{96,0},{1,33},{33,65},{65,97},{97,1},{2,34}... | collective-permute-start | bytes 589832 | tf_op jit(solution)/shard_map/ppermute | solution.py:23
  8.7 17.6 %collective-permute-start = (bf16[2,512,512]{2,1,0:T(8,128)(2,1)S(1)}, bf16[2,512,512]{2,1,0:T(8,128)(2,1)S(1)}, u32[]{:S(2)}, u32[]{:S(2)}) collective-permute-start(bf16[2,512,512]{2,1,0:T(8,128)(2,1)S(1)} %slice_bitcast_fusion), channel_id=1, source_target_pairs={{0,1},{1,2},{2,3},{3,4},{4,5},{5,6},{6,7},{7,8},{8,9},{9,10},{10,1... | collective-permute-start | bytes 3145736 | tf_op jit(solution)/shard_map/ppermute | solution.py:28
  15.5 38.7 %all-to-all-start = ((f32[32,16,128]{2,1,0:T(8,128)}), f32[32,16,128]{2,1,0:T(8,128)S(1)}, u32[]{:S(2)}, u32[]{:S(2)}) async-start(f32[32,16,128]{2,1,0:T(8,128)} %broadcast_in_dim.56), calls=%async_computation | async-start | bytes 524288 | tf_op jit(solution)/shard_map/all_to_all | solution.py:285
  24.2 1.6 %collective-permute-start.6 = (bf16[3,64,512]{2,1,0:T(8,128)(2,1)S(1)}, bf16[3,64,512]{2,1,0:T(8,128)(2,1)S(1)}, u32[]{:S(2)}, u32[]{:S(2)}) collective-permute-start(bf16[3,64,512]{2,1,0:T(8,128)(2,1)S(1)} %collective-permute-done.3.dc), channel_id=1, source_target_pairs={{0,1},{1,0},{2,3},{3,2},{4,5},{5,4},{6,7},{7,6},{8,9},{9,8},{10,11... | collective-permute-start | bytes 589832 | tf_op jit(solution)/shard_map/ppermute | solution.py:32
  24.5 1.5 %collective-permute-start.5 = (bf16[3,64,512]{2,1,0:T(8,128)(2,1)S(1)}, bf16[3,64,512]{2,1,0:T(8,128)(2,1)S(1)}, u32[]{:S(2)}, u32[]{:S(2)}) collective-permute-start(bf16[3,64,512]{2,1,0:T(8,128)(2,1)S(1)} %collective-permute-done.2.db), channel_id=1, source_target_pairs={{0,1},{1,0},{2,3},{3,2},{4,5},{5,4},{6,7},{7,6},{8,9},{9,8},{10,11... | collective-permute-start | bytes 589832 | tf_op jit(solution)/shard_map/ppermute | solution.py:32
  24.8 1.5 %collective-permute-start.4 = (bf16[3,64,512]{2,1,0:T(8,128)(2,1)S(1)}, bf16[3,64,512]{2,1,0:T(8,128)(2,1)S(1)}, u32[]{:S(2)}, u32[]{:S(2)}) collective-permute-start(bf16[3,64,512]{2,1,0:T(8,128)(2,1)S(1)} %collective-permute-done.1.da), channel_id=1, source_target_pairs={{0,1},{1,0},{2,3},{3,2},{4,5},{5,4},{6,7},{7,6},{8,9},{9,8},{10,11... | collective-permute-start | bytes 589832 | tf_op jit(solution)/shard_map/ppermute | solution.py:32
  26.3 27.9 %copy-start = (f32[512]{0:T(512)S(1)}, f32[512]{0:T(512)}, u32[]{:S(2)}) copy-start(f32[512]{0:T(512)} %param.10) | copy-start | bytes 6148

commit v4 on v3

--- a/solution.py
+++ b/solution.py
@@ -38,7 +38,7 @@
     return one, two, value - one - two
 
 
-def table_kernel(packed, rate, scaled, high, low, counts, E):
+def table_kernel(packed, rate, constants, high, low, counts, E):
     nall, lanes = packed.shape
     nchan = rate.shape[1]
     nlat = high.shape[0]
@@ -71,8 +71,9 @@
         hit = (jnp.broadcast_to(ids, (nall, lanes)) == me * per + i).astype(F32)
         counts[i : i + 1, :] = jnp.sum(hit, 0, keepdims=True)
     E[0:lanes, :] = table
+    scaled = constants[0 : high.shape[1], :]
     for j in range(nlat):
-        value = scaled[...] * E[j : j + 1, :]
+        value = scaled * E[j : j + 1, :]
         upper = value.astype(BF16)
         high[j] = upper
         low[j] = (value - upper.astype(F32)).astype(BF16)
@@ -107,24 +108,26 @@
 
 
 def conv_kernel(
-    window, keep, x_hbm, halo_hbm, own_w, da, db, dc, sa, sb, sc, decay, scaled,
-    feat_hbm, last, sums, w, X, HA, HB, FA, FB, R, pooled, wsem, insem, outsem, *, shards,
+    window, packing, x_hbm, halo_hbm, mine, da, db, dc, so, sa, sb, sc, constants,
+    feat_hbm, last, sums, w, X, HA, HB, FA, FB, R, pooled, kept, wsem, insem, outsem, *, shards,
 ):
     nframe, npos, nchan = x_hbm.shape
     tiles, groups = npos // TILE, nframe // GROUP
     total = tiles * groups
     H, F = (HA, HB), (FA, FB)
-    half, depth = da.shape[1], own_w.shape[1]
+    half = da.shape[1]
+    depth = 2 * half
+    nproj = sums.shape[0] // 3
     me = lax.axis_index("dp")
     side = lax.rem(lax.axis_index("tm"), 2)
     lead = KT - 1
 
     def weights():
-        copies = [pltpu.make_async_copy(own_w, w.at[:, pl.ds(pl.multiple_of(me * depth, depth), depth)], wsem.at[0])]
-        slot = 1
-        for step, mine, other in ((shards - 1, da, sa), (1, db, sb), (2, dc, sc)):
+        copies = []
+        slot = 0
+        for step, near, far in ((0, mine, so), (shards - 1, da, sa), (1, db, sb), (2, dc, sc)):
             base = lax.rem(me + step, shards) * depth
-            for piece, lane in ((mine, side), (other, 1 - side)):
+            for piece, lane in ((near, side), (far, 1 - side)):
                 row = pl.multiple_of(base + lane * half, half)
                 copies.append(pltpu.make_async_copy(piece, w.at[:, pl.ds(row, half)], wsem.at[slot]))
                 slot += 1
@@ -173,7 +176,7 @@
             scale = R[g * TILE + r : g * TILE + r + SUB, :]
             v = F[s][g, r : r + SUB, :].astype(F32)
             v = jnp.concatenate([v[:, n : n + 128] * scale for n in range(0, nchan, 128)], 1)
-            state = state * (decay[...] * keep[f + g]) + v
+            state = state * kept[pl.ds(f + g, 1), :] + v
             pooled[window[f + g], rows, :] += state
         last[rows, :] = state
 
@@ -196,6 +199,7 @@
     for q in range(tiles):
         prior(q).start()
         entering(q).start()
+    kept[...] = constants[nproj : nproj + 1, :] * packing[:, 0:1]
     last[...] = jnp.zeros_like(last)
     pooled[...] = jnp.zeros_like(pooled)
     for copy in pieces:
@@ -227,8 +231,7 @@
         return 0
 
     lax.fori_loop(0, total // 2, body, 0)
-    nproj = scaled.shape[0]
-    upper, lower = split(scaled[...])
+    upper, lower = split(constants[0:nproj, :])
     both = jnp.concatenate([upper, lower], 0)
     for j in range(3):
         top, rest = split(pooled[j])
@@ -268,25 +271,25 @@
     side = me % 2
     x = clips[0]
 
-    own_w = w_time * jnp.asarray(0.5, BF16)
-    half = own_w.shape[1] // 2
-    mine = lax.dynamic_slice_in_dim(own_w, side * half, half, 1)
+    half = w_time.shape[1] // 2
+    mine = lax.dynamic_slice_in_dim(w_time, side * half, half, 1) * jnp.asarray(0.5, BF16)
     dc = rotated(mine, "dp", 2)
     da = rotated(mine, "dp", 1)
     db = rotated(mine, "dp", -1)
+    so = swapped(mine, "tm")
     sa, sb, sc = swapped(da, "tm"), swapped(db, "tm"), swapped(dc, "tm")
     rate, gain, w_lat, _ = lax.optimization_barrier((rate, gain, w_lat, mine))
     halo = shifted(x[nframe - (KT - 1) :], "tm", 1)
     window = latent_ids - me.astype(jnp.int32) * per
-    keep = jnp.where(latent_ids < 0, 0.0, keep)
     lane = jnp.arange(128, dtype=jnp.int32)[None]
-    local = jnp.where(lane < 64, keep[:, None], latent_ids.astype(F32)[:, None])
-    local = jnp.broadcast_to(local[None], (ndev, nframe, 128))
+    packing = jnp.where(lane < 64, keep[:, None], latent_ids.astype(F32)[:, None])
+    local = jnp.broadcast_to(packing[None], (ndev, nframe, 128))
     packed = lax.all_to_all(local, "tm", 0, 0).reshape(nall, 128)
 
-    decay = jnp.exp(-rate)[None]
     inject = jnp.sqrt(-jnp.expm1(-2.0 * rate))
-    scaled = w_lat.T.astype(F32) * (inject * gain)[None]
+    row = jnp.arange(nproj + 8, dtype=jnp.int32)[:, None]
+    padded = jnp.pad(w_lat.T.astype(F32), ((0, 8), (0, 0)))
+    constants = jnp.where(row < nproj, padded * (inject * gain)[None], jnp.exp(-rate)[None])
 
     vmem = pl.BlockSpec(memory_space=pltpu.VMEM)
     smem = pl.BlockSpec(memory_space=pltpu.SMEM)
@@ -301,7 +304,7 @@
             jax.ShapeDtypeStruct((npos, nchan), F32),
             jax.ShapeDtypeStruct((3 * nproj, npos), F32),
         ),
-        in_specs=[smem, smem] + [hbm] * 9 + [vmem] * 2,
+        in_specs=[smem, vmem] + [hbm] * 10 + [vmem],
         out_specs=(hbm, vmem, vmem),
         scratch_shapes=[
             pltpu.VMEM((KT, nchan, nchan), BF16),
@@ -312,7 +315,8 @@
             pltpu.VMEM((GROUP, TILE, nchan), BF16),
             pltpu.VMEM((stage_rows, 128), F32),
             pltpu.VMEM((3, npos, nchan), F32),
-            pltpu.SemaphoreType.DMA((7,)),
+            pltpu.VMEM((nframe, nchan), F32),
+            pltpu.SemaphoreType.DMA((8,)),
             pltpu.SemaphoreType.DMA((2 * npos // TILE,)),
             pltpu.SemaphoreType.DMA((2,)),
         ],
@@ -324,7 +328,7 @@
         ),
         name="conv",
     )
-    features, last, own = conv(window, keep, x, halo, own_w, da, db, dc, sa, sb, sc, decay, scaled)
+    features, last, own = conv(window, packing, x, halo, mine, da, db, dc, so, sa, sb, sc, constants)
     packed, last = lax.optimization_barrier((packed, last))
     high, low, counts = pl.pallas_call(
         table_kernel,
@@ -337,7 +341,7 @@
             flops=12 * nlat * nall * nchan, bytes_accessed=4 << 20, transcendentals=nall * nchan
         ),
         name="tables",
-    )(packed, rate[None], scaled)
+    )(packed, rate[None], constants)
     sends = pl.pallas_call(
         spread_kernel,
         out_shape=jax.ShapeDtypeStruct((ndev, per * nproj, npos), BF16),

time: 85.5 us -> 84.7 us (level)
    ppermute x3 -> x4, starting transfers between devices: 0.83 us -> 2.29 us  [swapped(): lax.ppermute(value, axis, [(s, s ^ 1) for s in range(lax.axis_size(axis))])]
    mul x3 -> x2, other arithmetic: 2.47 us -> 1.69 us  [the longest x1 0.97 us: per_device(): lax.dynamic_slice_in_dim(w_time, side * half, half, 1)]
  transfers between devices with their start and end apart: 8 -> 9, of which waited for: 2 -> 2; matrix products, arithmetic and copies ran while one was open for 6% -> 6% of each run, Pallas kernels for 33% -> 33%
where the time goes in v4:
time: 84.7 us; the launch traced here: 84.3 us
  Pallas kernels  31.9 us (38%)
  blocking collectives  26.7 us (32%)
  starting transfers between devices  18.5 us (22%)
  other arithmetic  3.95 us (5%)
  local copies, waits for them, and re-layouts  2.02 us (2%)
    pallas_call x1, Pallas kernels, per_device(): conv(window, packing, x, halo, mine, da, db, dc, so, sa, sb, sc, constants)  27.7 us
    all_to_all x1, blocking collectives, per_device(): outs = [lax.all_to_all(sends, 'tm', 0, 0), own]  26.7 us
    all_to_all x1, starting transfers between devices, per_device(): packed = lax.all_to_all(local, 'tm', 0, 0).reshape(nall, 128)  7.92 us
    ppermute x3, starting transfers between devices, rotated(): lax.ppermute(value, axis, [(s, (s + steps) % count) for s in range(count)])  4.32 us
    ppermute x1, starting transfers between devices, shifted(): lax.ppermute(value, axis, [(s, s + steps) for s in range(count - steps)])  4.02 us
    ppermute x4, starting transfers between devices, swapped(): lax.ppermute(value, axis, [(s, s ^ 1) for s in range(lax.axis_size(axis))])  2.29 us
    pallas_call x1, Pallas kernels, per_device(): pl.pallas_call(spread_kernel, out_shape=jax.ShapeDtypeStruct((ndev, per *...  1.84 us
  transfers between devices with their start and end apart: 9, of which 2 were waited for; matrix products, arithmetic and copies ran while one was open for 6% of the time, Pallas kernels for 33%

profile of v4, /device:TPU:1, one launch (start us, length us, event | category | flops | bytes accessed | tf_op | source)
XLA Modules:
  0.0 84.3 jit_solution(7796317624466024693)
XLA Ops:
  0.6 1.0 %dynamic-slice_multiply_fusion.mine = bf16[3,64,512]{2,1,0:T(8,128)(2,1)S(1)} fusion(bf16[3,128,512]{2,1,0:T(8,128)(2,1)} %param.8, s32[]{:T(128)S(6)} %select_n.20), kind=kLoop, calls=%fused_computation.1 | loop fusion | flops 393216 | bytes 393220 | tf_op jit(solution)/shard_map/mul | solution.py:275
  1.6 1.5 %collective-permute-start.4 = (bf16[3,64,512]{2,1,0:T(8,128)(2,1)S(1)}, bf16[3,64,512]{2,1,0:T(8,128)(2,1)S(1)}, u32[]{:S(2)}, u32[]{:S(2)}) collective-permute-start(bf16[3,64,512]{2,1,0:T(8,128)(2,1)S(1)} %dynamic-slice_multiply_fusion.mine), channel_id=1, source_target_pairs={{0,1},{1,0},{2,3},{3,2},{4,5},{5,4},{6,7},{7,6},{8,9},{9,8},{10,11... | collective-permute-start | bytes 589832 | tf_op jit(solution)/shard_map/ppermute | solution.py:32
  3.1 2.9 %collective-permute-start.3 = (bf16[3,64,512]{2,1,0:T(8,128)(2,1)S(1)}, bf16[3,64,512]{2,1,0:T(8,128)(2,1)S(1)}, u32[]{:S(2)}, u32[]{:S(2)}) collective-permute-start(bf16[3,64,512]{2,1,0:T(8,128)(2,1)S(1)} %dynamic-slice_multiply_fusion.mine), channel_id=1, source_target_pairs={{0,64},{32,96},{64,0},{96,32},{1,65},{33,97},{65,1},{97,33},{2,66}... | collective-permute-start | bytes 589832 | tf_op jit(solution)/shard_map/ppermute | solution.py:23
  5.9 0.9 %collective-permute-start.2 = (bf16[3,64,512]{2,1,0:T(8,128)(2,1)S(1)}, bf16[3,64,512]{2,1,0:T(8,128)(2,1)S(1)}, u32[]{:S(2)}, u32[]{:S(2)}) collective-permute-start(bf16[3,64,512]{2,1,0:T(8,128)(2,1)S(1)} %dynamic-slice_multiply_fusion.mine), channel_id=1, source_target_pairs={{0,96},{32,0},{64,32},{96,64},{1,97},{33,1},{65,33},{97,65},{2,98}... | collective-permute-start | bytes 589832 | tf_op jit(solution)/shard_map/ppermute | solution.py:23
  6.8 0.6 collective-permute-start.1
  7.4 1.3 %slice_bitcast_fusion = bf16[2,512,512]{2,1,0:T(8,128)(2,1)S(1)} fusion(bf16[1,16,512,512]{3,2,1,0:T(8,128)(2,1)} %param.7), kind=kLoop, calls=%fused_computation | loop fusion | bytes 2097152 | tf_op jit(solution)/shard_map/slice | solution.py:282
  8.7 4.0 %collective-permute-start = (bf16[2,512,512]{2,1,0:T(8,128)(2,1)S(1)}, bf16[2,512,512]{2,1,0:T(8,128)(2,1)S(1)}, u32[]{:S(2)}, u32[]{:S(2)}) collective-permute-start(bf16[2,512,512]{2,1,0:T(8,128)(2,1)S(1)} %slice_bitcast_fusion), channel_id=1, source_target_pairs={{0,1},{1,2},{2,3},{3,4},{4,5},{5,6},{6,7},{7,8},{8,9},{9,10},{10,1... | collective-permute-start | bytes 3145736 | tf_op jit(solution)/shard_map/ppermute | solution.py:28
  12.7 0.7 fusion
  13.5 0.7 broadcast_select_fusion.packing
  14.2 0.7 broadcast_in_dim.67
  14.9 7.9 %all-to-all-start = ((f32[32,16,128]{2,1,0:T(8,128)}), f32[32,16,128]{2,1,0:T(8,128)S(1)}, u32[]{:S(2)}, u32[]{:S(2)}) async-start(f32[32,16,128]{2,1,0:T(8,128)} %broadcast_in_dim.67), calls=%async_computation | async-start | bytes 524288 | tf_op jit(solution)/shard_map/all_to_all | solution.py:287
  22.9 0.7 sqrt_multiply_fusion
  23.6 0.0 collective-permute-done.3.dc
  23.6 0.3 collective-permute-start.7
  23.9 0.0 collective-permute-done.2.db
  23.9 0.3 collective-permute-start.6
  24.2 0.0 collective-permute-done.1.da
  24.2 0.2 collective-permute-start.5
  24.4 0.8 multiply_select_fusion.constants
  25.2 0.0 collective-permute-done.4.so
  25.2 0.0 collective-permute-done.7.sc
  25.2 0.2 collective-permute-done.6.sb
  25.4 0.3 collective-permute-done.5.sa
  25.7 0.0 collective-permute-done.halo_hbm
  25.7 0.0 copy-start
  25.7 27.7 %conv.1 = (bf16[16,512,512]{2,1,0:T(8,128)(2,1)}, f32[512,512]{1,0:T(8,128)S(1)}, f32[48,512]{1,0:T(8,128)S(1)}) custom-call(s32[16]{0:T(128)S(1)} %get-tuple-element.27.window, f32[16,128]{1,0:T(8,128)S(1)} %broadcast_select_fusion.packing, bf16[16,512,512]{2,1,0:T(8,128)(2,1)} %bitcast.10, bf16[2,512,512]{2,1,0:T(8,128)(2,1)S(1)} %collective-permute-done.halo_hbm, ...), custom_call_target="tpu_custom_call" | custom-call | flops 12884901888 | bytes 16777216 | tf_op jit(solution)/shard_map/conv/pallas_call | solution.py:331
  53.4 0.0 all-to-all-done
  53.4 0.0 copy-done
  53.5 1.6 %tables.1 = (bf16[64,16,512]{2,1,0:T(8,128)(2,1)S(1)}, bf16[64,16,512]{2,1,0:T(8,128)(2,1)S(1)}, f32[2,128]{1,0:T(2,128)S(1)}) custom-call(f32[512,128]{1,0:T(8,128)S(1)} %bitcast.8, f32[1,512]{1,0:T(1,128)S(1)} %bitcast.9, f32[24,512]{1,0:T(8,128)S(1)} %multiply_select_fusion.constants), custom_call_target="tpu_custom_call" | custom-call | flops 201326592 | bytes 4194304 | tf_op jit(solution)/shard_map/tables/pallas_call | solution.py:333
  55.0 1.8 %spread.1 = bf16[32,32,512]{2,1,0:T(8,128)(2,1)S(1)} custom-call(bf16[64,16,512]{2,1,0:T(8,128)(2,1)S(1)} %get-tuple-element.20.high, bf16[64,16,512]{2,1,0:T(8,128)(2,1)S(1)} %get-tuple-element.21.low, f32[512,512]{1,0:T(8,128)S(1)} %get-tuple-element.22.last, f32[48,512]{1,0:T(8,128)S(1)} %get-tuple-element.23.own.refs_1_), custom_call_target="tpu_custom_call" | custom-call | tf_op jit(solution)/shard_map/spread/pallas_call | solution.py:345
  56.9 26.7 %all_to_all.10.refs_0_ = bf16[32,32,512]{2,1,0:T(8,128)(2,1)S(1)} all-to-all(bf16[32,32,512]{2,1,0:T(8,128)(2,1)S(1)} %spread.1), channel_id=1, replica_groups=mesh['dp'=4,'tm'=32] {'tm'}, dimensions={0} | all-to-all | bytes 2097152 | tf_op jit(solution)/shard_map/all_to_all | solution.py:353
  83.5 0.8 final.1
  (2 shorter events, 0.0 us)
Async XLA Ops:
  1.6 23.6 %collective-permute-start.4 = (bf16[3,64,512]{2,1,0:T(8,128)(2,1)S(1)}, bf16[3,64,512]{2,1,0:T(8,128)(2,1)S(1)}, u32[]{:S(2)}, u32[]{:S(2)}) collective-permute-start(bf16[3,64,512]{2,1,0:T(8,128)(2,1)S(1)} %dynamic-slice_multiply_fusion.mine), channel_id=1, source_target_pairs={{0,1},{1,0},{2,3},{3,2},{4,5},{5,4},{6,7},{7,6},{8,9},{9,8},{10,11... | collective-permute-start | bytes 589832 | tf_op jit(solution)/shard_map/ppermute | solution.py:32
  3.1 20.5 %collective-permute-start.3 = (bf16[3,64,512]{2,1,0:T(8,128)(2,1)S(1)}, bf16[3,64,512]{2,1,0:T(8,128)(2,1)S(1)}, u32[]{:S(2)}, u32[]{:S(2)}) collective-permute-start(bf16[3,64,512]{2,1,0:T(8,128)(2,1)S(1)} %dynamic-slice_multiply_fusion.mine), channel_id=1, source_target_pairs={{0,64},{32,96},{64,0},{96,32},{1,65},{33,97},{65,1},{97,33},{2,66}... | collective-permute-start | bytes 589832 | tf_op jit(solution)/shard_map/ppermute | solution.py:23
  5.9 18.0 %collective-permute-start.2 = (bf16[3,64,512]{2,1,0:T(8,128)(2,1)S(1)}, bf16[3,64,512]{2,1,0:T(8,128)(2,1)S(1)}, u32[]{:S(2)}, u32[]{:S(2)}) collective-permute-start(bf16[3,64,512]{2,1,0:T(8,128)(2,1)S(1)} %dynamic-slice_multiply_fusion.mine), channel_id=1, source_target_pairs={{0,96},{32,0},{64,32},{96,64},{1,97},{33,1},{65,33},{97,65},{2,98}... | collective-permute-start | bytes 589832 | tf_op jit(solution)/shard_map/ppermute | solution.py:23
  6.8 17.4 %collective-permute-start.1 = (bf16[3,64,512]{2,1,0:T(8,128)(2,1)S(1)}, bf16[3,64,512]{2,1,0:T(8,128)(2,1)S(1)}, u32[]{:S(2)}, u32[]{:S(2)}) collective-permute-start(bf16[3,64,512]{2,1,0:T(8,128)(2,1)S(1)} %dynamic-slice_multiply_fusion.mine), channel_id=1, source_target_pairs={{0,32},{32,64},{64,96},{96,0},{1,33},{33,65},{65,97},{97,1},{2,34}... | collective-permute-start | bytes 589832 | tf_op jit(solution)/shard_map/ppermute | solution.py:23
  8.7 17.0 %collective-permute-start = (bf16[2,512,512]{2,1,0:T(8,128)(2,1)S(1)}, bf16[2,512,512]{2,1,0:T(8,128)(2,1)S(1)}, u32[]{:S(2)}, u32[]{:S(2)}) collective-permute-start(bf16[2,512,512]{2,1,0:T(8,128)(2,1)S(1)} %slice_bitcast_fusion), channel_id=1, source_target_pairs={{0,1},{1,2},{2,3},{3,4},{4,5},{5,6},{6,7},{7,8},{8,9},{9,10},{10,1... | collective-permute-start | bytes 3145736 | tf_op jit(solution)/shard_map/ppermute | solution.py:28
  14.9 38.5 %all-to-all-start = ((f32[32,16,128]{2,1,0:T(8,128)}), f32[32,16,128]{2,1,0:T(8,128)S(1)}, u32[]{:S(2)}, u32[]{:S(2)}) async-start(f32[32,16,128]{2,1,0:T(8,128)} %broadcast_in_dim.67), calls=%async_computation | async-start | bytes 524288 | tf_op jit(solution)/shard_map/all_to_all | solution.py:287
  23.6 1.6 %collective-permute-start.7 = (bf16[3,64,512]{2,1,0:T(8,128)(2,1)S(1)}, bf16[3,64,512]{2,1,0:T(8,128)(2,1)S(1)}, u32[]{:S(2)}, u32[]{:S(2)}) collective-permute-start(bf16[3,64,512]{2,1,0:T(8,128)(2,1)S(1)} %collective-permute-done.3.dc), channel_id=1, source_target_pairs={{0,1},{1,0},{2,3},{3,2},{4,5},{5,4},{6,7},{7,6},{8,9},{9,8},{10,11... | collective-permute-start | bytes 589832 | tf_op jit(solution)/shard_map/ppermute | solution.py:32
  23.9 1.5 %collective-permute-start.6 = (bf16[3,64,512]{2,1,0:T(8,128)(2,1)S(1)}, bf16[3,64,512]{2,1,0:T(8,128)(2,1)S(1)}, u32[]{:S(2)}, u32[]{:S(2)}) collective-permute-start(bf16[3,64,512]{2,1,0:T(8,128)(2,1)S(1)} %collective-permute-done.2.db), channel_id=1, source_target_pairs={{0,1},{1,0},{2,3},{3,2},{4,5},{5,4},{6,7},{7,6},{8,9},{9,8},{10,11... | collective-permute-start | bytes 589832 | tf_op jit(solution)/shard_map/ppermute | solution.py:32
  24.2 1.5 %collective-permute-start.5 = (bf16[3,64,512]{2,1,0:T(8,128)(2,1)S(1)}, bf16[3,64,512]{2,1,0:T(8,128)(2,1)S(1)}, u32[]{:S(2)}, u32[]{:S(2)}) collective-permute-start(bf16[3,64,512]{2,1,0:T(8,128)(2,1)S(1)} %collective-permute-done.1.da), channel_id=1, source_target_pairs={{0,1},{1,0},{2,3},{3,2},{4,5},{5,4},{6,7},{7,6},{8,9},{9,8},{10,11... | collective-permute-start | bytes 589832 | tf_op jit(solution)/shard_map/ppermute | solution.py:32
  25.7 27.8 %copy-start = (f32[512]{0:T(512)S(1)}, f32[512]{0:T(512)}, u32[]{:S(2)}) copy-start(f32[512]{0:T(512)} %param.10) | copy-start | bytes 6148

commit v5 on v4

--- a/solution.py
+++ b/solution.py
@@ -142,6 +142,8 @@
         return pltpu.make_async_copy(halo_hbm.at[:, part], X.at[0:lead, part], insem.at[tiles + q])
 
     def place(i):
+        if isinstance(i, int):
+            return i // groups * TILE, i % groups * GROUP
         return pl.multiple_of(i // groups * TILE, TILE), lax.rem(i, groups) * GROUP
 
     def leaving(i, s):
@@ -182,9 +184,18 @@
 
     products = [(m, n) for m in range(GROUP * TILE // ROWS) for n in range(0, nchan, 256)]
 
+    def project(q):
+        part = slice(q * TILE, (q + 1) * TILE)
+        upper, lower = split(constants[0:nproj, :])
+        both = jnp.concatenate([upper, lower], 0)
+        for j in range(3):
+            top, rest = split(pooled[j, part, :])
+            value = times(both, top)
+            sums[j * nproj : (j + 1) * nproj, part] = value[:nproj] + value[nproj:] + times(upper, rest)
+
     def stage(later, ls, i, s):
         work = [(g, r) for r in range(0, TILE, SUB) for g in range(GROUP)] + [(None, r) for r in range(0, TILE, SUB)]
-        todo = list(products)
+        todo = [] if later is None else list(products)
         for at, (g, r) in enumerate(work):
             if todo and at * len(products) // len(work) >= len(products) - len(todo):
                 product(later, ls, *todo.pop(0))
@@ -226,17 +237,20 @@
             prior(q).wait()
             entering(q).wait()
 
-        stage(lax.rem(i + 2, total), 0, i + 1, 1)
+        stage(i + 2, 0, i + 1, 1)
         leaving(i + 1, 1).start()
         return 0
 
-    lax.fori_loop(0, total // 2, body, 0)
-    upper, lower = split(constants[0:nproj, :])
-    both = jnp.concatenate([upper, lower], 0)
-    for j in range(3):
-        top, rest = split(pooled[j])
-        part = times(both, top)
-        sums[j * nproj : (j + 1) * nproj, :] = part[:nproj] + part[nproj:] + times(upper, rest)
+    lax.fori_loop(0, total // 2 - 1, body, 0)
+    leaving(total - 4, 0).wait()
+    leaving(total - 3, 1).wait()
+    stage(total - 1, 1, total - 2, 0)
+    leaving(total - 2, 0).start()
+    for q in range(tiles - 1):
+        project(q)
+    stage(None, None, total - 1, 1)
+    leaving(total - 1, 1).start()
+    project(tiles - 1)
     leaving(total - 2, 0).wait()
     leaving(total - 1, 1).wait()
 

time: 84.7 us -> 84.2 us (level)
  transfers between devices with their start and end apart: 9 -> 9, of which waited for: 2 -> 2; matrix products, arithmetic and copies ran while one was open for 6% -> 6% of each run, Pallas kernels for 33% -> 32%
where the time goes in v5:
time: 84.2 us; the launch traced here: 83.8 us
  Pallas kernels  31.4 us (37%)
  blocking collectives  26.7 us (32%)
  starting transfers between devices  18.5 us (22%)
  other arithmetic  3.95 us (5%)
  local copies, waits for them, and re-layouts  2.02 us (2%)
    pallas_call x1, Pallas kernels, per_device(): conv(window, packing, x, halo, mine, da, db, dc, so, sa, sb, sc, constants)  27.2 us
    all_to_all x1, blocking collectives, per_device(): outs = [lax.all_to_all(sends, 'tm', 0, 0), own]  26.7 us
    all_to_all x1, starting transfers between devices, per_device(): packed = lax.all_to_all(local, 'tm', 0, 0).reshape(nall, 128)  7.92 us
    ppermute x3, starting transfers between devices, rotated(): lax.ppermute(value, axis, [(s, (s + steps) % count) for s in range(count)])  4.32 us
    ppermute x1, starting transfers between devices, shifted(): lax.ppermute(value, axis, [(s, s + steps) for s in range(count - steps)])  4.02 us
    ppermute x4, starting transfers between devices, swapped(): lax.ppermute(value, axis, [(s, s ^ 1) for s in range(lax.axis_size(axis))])  2.29 us
    pallas_call x1, Pallas kernels, per_device(): pl.pallas_call(spread_kernel, out_shape=jax.ShapeDtypeStruct((ndev, per *...  1.84 us
  transfers between devices with their start and end apart: 9, of which 2 were waited for; matrix products, arithmetic and copies ran while one was open for 6% of the time, Pallas kernels for 32%

profile of v5, /device:TPU:1, one launch (start us, length us, event | category | flops | bytes accessed | tf_op | source)
XLA Modules:
  0.0 83.8 jit_solution(6893051037869208401)
XLA Ops:
  0.6 1.0 %dynamic-slice_multiply_fusion.mine = bf16[3,64,512]{2,1,0:T(8,128)(2,1)S(1)} fusion(bf16[3,128,512]{2,1,0:T(8,128)(2,1)} %param.8, s32[]{:T(128)S(6)} %select_n.20), kind=kLoop, calls=%fused_computation.1 | loop fusion | flops 393216 | bytes 393220 | tf_op jit(solution)/shard_map/mul | solution.py:289
  1.6 1.5 %collective-permute-start.4 = (bf16[3,64,512]{2,1,0:T(8,128)(2,1)S(1)}, bf16[3,64,512]{2,1,0:T(8,128)(2,1)S(1)}, u32[]{:S(2)}, u32[]{:S(2)}) collective-permute-start(bf16[3,64,512]{2,1,0:T(8,128)(2,1)S(1)} %dynamic-slice_multiply_fusion.mine), channel_id=1, source_target_pairs={{0,1},{1,0},{2,3},{3,2},{4,5},{5,4},{6,7},{7,6},{8,9},{9,8},{10,11... | collective-permute-start | bytes 589832 | tf_op jit(solution)/shard_map/ppermute | solution.py:32
  3.1 2.9 %collective-permute-start.3 = (bf16[3,64,512]{2,1,0:T(8,128)(2,1)S(1)}, bf16[3,64,512]{2,1,0:T(8,128)(2,1)S(1)}, u32[]{:S(2)}, u32[]{:S(2)}) collective-permute-start(bf16[3,64,512]{2,1,0:T(8,128)(2,1)S(1)} %dynamic-slice_multiply_fusion.mine), channel_id=1, source_target_pairs={{0,64},{32,96},{64,0},{96,32},{1,65},{33,97},{65,1},{97,33},{2,66}... | collective-permute-start | bytes 589832 | tf_op jit(solution)/shard_map/ppermute | solution.py:23
  5.9 0.9 %collective-permute-start.2 = (bf16[3,64,512]{2,1,0:T(8,128)(2,1)S(1)}, bf16[3,64,512]{2,1,0:T(8,128)(2,1)S(1)}, u32[]{:S(2)}, u32[]{:S(2)}) collective-permute-start(bf16[3,64,512]{2,1,0:T(8,128)(2,1)S(1)} %dynamic-slice_multiply_fusion.mine), channel_id=1, source_target_pairs={{0,96},{32,0},{64,32},{96,64},{1,97},{33,1},{65,33},{97,65},{2,98}... | collective-permute-start | bytes 589832 | tf_op jit(solution)/shard_map/ppermute | solution.py:23
  6.8 0.6 collective-permute-start.1
  7.4 1.3 %slice_bitcast_fusion = bf16[2,512,512]{2,1,0:T(8,128)(2,1)S(1)} fusion(bf16[1,16,512,512]{3,2,1,0:T(8,128)(2,1)} %param.7), kind=kLoop, calls=%fused_computation | loop fusion | bytes 2097152 | tf_op jit(solution)/shard_map/slice | solution.py:296
  8.7 4.0 %collective-permute-start = (bf16[2,512,512]{2,1,0:T(8,128)(2,1)S(1)}, bf16[2,512,512]{2,1,0:T(8,128)(2,1)S(1)}, u32[]{:S(2)}, u32[]{:S(2)}) collective-permute-start(bf16[2,512,512]{2,1,0:T(8,128)(2,1)S(1)} %slice_bitcast_fusion), channel_id=1, source_target_pairs={{0,1},{1,2},{2,3},{3,4},{4,5},{5,6},{6,7},{7,8},{8,9},{9,10},{10,1... | collective-permute-start | bytes 3145736 | tf_op jit(solution)/shard_map/ppermute | solution.py:28
  12.7 0.7 fusion
  13.5 0.7 broadcast_select_fusion.packing
  14.2 0.7 broadcast_in_dim.67
  14.9 7.9 %all-to-all-start = ((f32[32,16,128]{2,1,0:T(8,128)}), f32[32,16,128]{2,1,0:T(8,128)S(1)}, u32[]{:S(2)}, u32[]{:S(2)}) async-start(f32[32,16,128]{2,1,0:T(8,128)} %broadcast_in_dim.67), calls=%async_computation | async-start | bytes 524288 | tf_op jit(solution)/shard_map/all_to_all | solution.py:301
  22.9 0.7 sqrt_multiply_fusion
  23.6 0.0 collective-permute-done.3.dc
  23.6 0.3 collective-permute-start.7
  23.9 0.0 collective-permute-done.2.db
  23.9 0.3 collective-permute-start.6
  24.2 0.0 collective-permute-done.1.da
  24.2 0.2 collective-permute-start.5
  24.4 0.8 multiply_select_fusion.constants
  25.2 0.0 collective-permute-done.4.so
  25.2 0.0 collective-permute-done.7.sc
  25.2 0.2 collective-permute-done.6.sb
  25.4 0.3 collective-permute-done.5.sa
  25.7 0.0 collective-permute-done.halo_hbm
  25.7 0.0 copy-start
  25.7 27.2 %conv.1 = (bf16[16,512,512]{2,1,0:T(8,128)(2,1)}, f32[512,512]{1,0:T(8,128)S(1)}, f32[48,512]{1,0:T(8,128)S(1)}) custom-call(s32[16]{0:T(128)S(1)} %get-tuple-element.27.window, f32[16,128]{1,0:T(8,128)S(1)} %broadcast_select_fusion.packing, bf16[16,512,512]{2,1,0:T(8,128)(2,1)} %bitcast.10, bf16[2,512,512]{2,1,0:T(8,128)(2,1)S(1)} %collective-permute-done.halo_hbm, ...), custom_call_target="tpu_custom_call" | custom-call | flops 12884901888 | bytes 16777216 | tf_op jit(solution)/shard_map/conv/pallas_call | solution.py:345
  52.9 0.0 all-to-all-done
  52.9 0.0 copy-done
  52.9 1.6 %tables.1 = (bf16[64,16,512]{2,1,0:T(8,128)(2,1)S(1)}, bf16[64,16,512]{2,1,0:T(8,128)(2,1)S(1)}, f32[2,128]{1,0:T(2,128)S(1)}) custom-call(f32[512,128]{1,0:T(8,128)S(1)} %bitcast.8, f32[1,512]{1,0:T(1,128)S(1)} %bitcast.9, f32[24,512]{1,0:T(8,128)S(1)} %multiply_select_fusion.constants), custom_call_target="tpu_custom_call" | custom-call | flops 201326592 | bytes 4194304 | tf_op jit(solution)/shard_map/tables/pallas_call | solution.py:347
  54.4 1.8 %spread.1 = bf16[32,32,512]{2,1,0:T(8,128)(2,1)S(1)} custom-call(bf16[64,16,512]{2,1,0:T(8,128)(2,1)S(1)} %get-tuple-element.20.high, bf16[64,16,512]{2,1,0:T(8,128)(2,1)S(1)} %get-tuple-element.21.low, f32[512,512]{1,0:T(8,128)S(1)} %get-tuple-element.22.last, f32[48,512]{1,0:T(8,128)S(1)} %get-tuple-element.23.own.refs_1_), custom_call_target="tpu_custom_call" | custom-call | tf_op jit(solution)/shard_map/spread/pallas_call | solution.py:359
  56.3 26.7 %all_to_all.10.refs_0_ = bf16[32,32,512]{2,1,0:T(8,128)(2,1)S(1)} all-to-all(bf16[32,32,512]{2,1,0:T(8,128)(2,1)S(1)} %spread.1), channel_id=1, replica_groups=mesh['dp'=4,'tm'=32] {'tm'}, dimensions={0} | all-to-all | bytes 2097152 | tf_op jit(solution)/shard_map/all_to_all | solution.py:367
  83.0 0.8 final.1
  (2 shorter events, 0.0 us)
Async XLA Ops:
  1.6 23.6 %collective-permute-start.4 = (bf16[3,64,512]{2,1,0:T(8,128)(2,1)S(1)}, bf16[3,64,512]{2,1,0:T(8,128)(2,1)S(1)}, u32[]{:S(2)}, u32[]{:S(2)}) collective-permute-start(bf16[3,64,512]{2,1,0:T(8,128)(2,1)S(1)} %dynamic-slice_multiply_fusion.mine), channel_id=1, source_target_pairs={{0,1},{1,0},{2,3},{3,2},{4,5},{5,4},{6,7},{7,6},{8,9},{9,8},{10,11... | collective-permute-start | bytes 589832 | tf_op jit(solution)/shard_map/ppermute | solution.py:32
  3.1 20.5 %collective-permute-start.3 = (bf16[3,64,512]{2,1,0:T(8,128)(2,1)S(1)}, bf16[3,64,512]{2,1,0:T(8,128)(2,1)S(1)}, u32[]{:S(2)}, u32[]{:S(2)}) collective-permute-start(bf16[3,64,512]{2,1,0:T(8,128)(2,1)S(1)} %dynamic-slice_multiply_fusion.mine), channel_id=1, source_target_pairs={{0,64},{32,96},{64,0},{96,32},{1,65},{33,97},{65,1},{97,33},{2,66}... | collective-permute-start | bytes 589832 | tf_op jit(solution)/shard_map/ppermute | solution.py:23
  5.9 18.0 %collective-permute-start.2 = (bf16[3,64,512]{2,1,0:T(8,128)(2,1)S(1)}, bf16[3,64,512]{2,1,0:T(8,128)(2,1)S(1)}, u32[]{:S(2)}, u32[]{:S(2)}) collective-permute-start(bf16[3,64,512]{2,1,0:T(8,128)(2,1)S(1)} %dynamic-slice_multiply_fusion.mine), channel_id=1, source_target_pairs={{0,96},{32,0},{64,32},{96,64},{1,97},{33,1},{65,33},{97,65},{2,98}... | collective-permute-start | bytes 589832 | tf_op jit(solution)/shard_map/ppermute | solution.py:23
  6.8 17.4 %collective-permute-start.1 = (bf16[3,64,512]{2,1,0:T(8,128)(2,1)S(1)}, bf16[3,64,512]{2,1,0:T(8,128)(2,1)S(1)}, u32[]{:S(2)}, u32[]{:S(2)}) collective-permute-start(bf16[3,64,512]{2,1,0:T(8,128)(2,1)S(1)} %dynamic-slice_multiply_fusion.mine), channel_id=1, source_target_pairs={{0,32},{32,64},{64,96},{96,0},{1,33},{33,65},{65,97},{97,1},{2,34}... | collective-permute-start | bytes 589832 | tf_op jit(solution)/shard_map/ppermute | solution.py:23
  8.7 17.0 %collective-permute-start = (bf16[2,512,512]{2,1,0:T(8,128)(2,1)S(1)}, bf16[2,512,512]{2,1,0:T(8,128)(2,1)S(1)}, u32[]{:S(2)}, u32[]{:S(2)}) collective-permute-start(bf16[2,512,512]{2,1,0:T(8,128)(2,1)S(1)} %slice_bitcast_fusion), channel_id=1, source_target_pairs={{0,1},{1,2},{2,3},{3,4},{4,5},{5,6},{6,7},{7,8},{8,9},{9,10},{10,1... | collective-permute-start | bytes 3145736 | tf_op jit(solution)/shard_map/ppermute | solution.py:28
  14.9 37.9 %all-to-all-start = ((f32[32,16,128]{2,1,0:T(8,128)}), f32[32,16,128]{2,1,0:T(8,128)S(1)}, u32[]{:S(2)}, u32[]{:S(2)}) async-start(f32[32,16,128]{2,1,0:T(8,128)} %broadcast_in_dim.67), calls=%async_computation | async-start | bytes 524288 | tf_op jit(solution)/shard_map/all_to_all | solution.py:301
  23.6 1.6 %collective-permute-start.7 = (bf16[3,64,512]{2,1,0:T(8,128)(2,1)S(1)}, bf16[3,64,512]{2,1,0:T(8,128)(2,1)S(1)}, u32[]{:S(2)}, u32[]{:S(2)}) collective-permute-start(bf16[3,64,512]{2,1,0:T(8,128)(2,1)S(1)} %collective-permute-done.3.dc), channel_id=1, source_target_pairs={{0,1},{1,0},{2,3},{3,2},{4,5},{5,4},{6,7},{7,6},{8,9},{9,8},{10,11... | collective-permute-start | bytes 589832 | tf_op jit(solution)/shard_map/ppermute | solution.py:32
  23.9 1.5 %collective-permute-start.6 = (bf16[3,64,512]{2,1,0:T(8,128)(2,1)S(1)}, bf16[3,64,512]{2,1,0:T(8,128)(2,1)S(1)}, u32[]{:S(2)}, u32[]{:S(2)}) collective-permute-start(bf16[3,64,512]{2,1,0:T(8,128)(2,1)S(1)} %collective-permute-done.2.db), channel_id=1, source_target_pairs={{0,1},{1,0},{2,3},{3,2},{4,5},{5,4},{6,7},{7,6},{8,9},{9,8},{10,11... | collective-permute-start | bytes 589832 | tf_op jit(solution)/shard_map/ppermute | solution.py:32
  24.2 1.5 %collective-permute-start.5 = (bf16[3,64,512]{2,1,0:T(8,128)(2,1)S(1)}, bf16[3,64,512]{2,1,0:T(8,128)(2,1)S(1)}, u32[]{:S(2)}, u32[]{:S(2)}) collective-permute-start(bf16[3,64,512]{2,1,0:T(8,128)(2,1)S(1)} %collective-permute-done.1.da), channel_id=1, source_target_pairs={{0,1},{1,0},{2,3},{3,2},{4,5},{5,4},{6,7},{7,6},{8,9},{9,8},{10,11... | collective-permute-start | bytes 589832 | tf_op jit(solution)/shard_map/ppermute | solution.py:32
  25.7 27.2 %copy-start = (f32[512]{0:T(512)S(1)}, f32[512]{0:T(512)}, u32[]{:S(2)}) copy-start(f32[512]{0:T(512)} %param.10) | copy-start | bytes 6148
